TPU v7x, 512 devices: a whole 4x8x8 slice. The times are simulated.
512 devices in a mesh: dp: 4 (over y_hi), ctx: 32 (over z, y_lo, core), head: 4 (over x).
Axes of the slice: x: 4, y: 8 (y_hi: 4, y_lo: 2; y = y_hi * 2 + y_lo), z: 8, core: 2. Of those that a mesh axis runs over, the one named last changes fastest.
Arguments:
- enc_query: bfloat16 [32768, 4096], P(('dp', 'ctx'), 'head'), parts along dimension 0, may hold values from -30 to 30
- enc_key: bfloat16 [32768, 4096], P(('dp', 'ctx'), 'head'), parts along dimension 0, may hold values from -6 to 6
- enc_value: bfloat16 [32768, 4096], P(('dp', 'ctx'), 'head'), parts along dimension 0, may hold values from -6 to 6
- doc_ids: int32 [32768], P(('dp', 'ctx')), parts along dimension 0, may hold values from 0 to 95, never falling along the last dimension, each value on 1 to 256 neighbouring positions
- key_map: bfloat16 [4096, 2048], P('ctx', 'head'), may hold values from -0.09375 to 0.09375
- value_map: bfloat16 [4096, 2048], P('ctx', 'head'), may hold values from -0.09375 to 0.09375
- tgt_query: bfloat16 [8192, 2048], P(('dp', 'ctx'), 'head'), parts along dimension 0, may hold values from -150 to 150
Outputs:
- cross_out: bfloat16 [8192, 2048], P(('dp', 'ctx'), 'head'), parts along dimension 0
There are 4 independent parts, one for each index of `dp`. A program takes and returns all parts, laid end to end along the dimension named above; an argument that names none is the same for every part. Nothing has to cross between parts.
Inputs may be any that keep to these rules, and one draw needn't show every extreme that they name: `doc_ids`: document ids never fall along the pack; each document holds 1 to 256 consecutive positions and one holds exactly 256.
All inputs are finite; a program needn't handle non-finite values.
Results may differ from a plain program's by a relative error of at most 0.011.
Values may be sent and summed in bfloat16 or wider, within the bound.
A program may use at most 64 MiB of HBM per device.

v0:
```python
import jax
import jax.numpy as jnp
from jax import lax
from jax.sharding import PartitionSpec as P

HEAD_DIM = 256


NEG_FILL = -1e30


def passed_along(value, axis, steps):
    count = lax.axis_size(axis)
    leading, last = (max(0, -steps), min(count, count - steps))
    return lax.ppermute(value, axis, [(source, source + steps) for source in range(leading, last)])


def masked_scores(query, keys, query_mark, key_mark):
    scale = query.shape[2] ** (-0.5)
    raw = jnp.einsum("rhe,khe->hrk", query, keys, preferred_element_type=jnp.float32) * scale
    same = query_mark[:, None] == key_mark[None, :]
    return jnp.where(same[None], raw, NEG_FILL)


def weighted(weights, values):
    return jnp.einsum(
        "hrk,khe->rhe", weights.astype(jnp.bfloat16), values, preferred_element_type=jnp.float32
    )


def normalize(summed, total):
    return summed / jnp.transpose(total)[:, :, None]


def dense_attend(query, keys, values, query_mark, key_mark):
    scores = masked_scores(query, keys, query_mark, key_mark)
    top = jnp.max(scores, axis=2, keepdims=True)
    weights = jnp.exp(scores - top)
    return normalize(weighted(weights, values), jnp.sum(weights, axis=2))


def on_device(enc_query, enc_key, enc_value, doc_ids, key_map, value_map, tgt_query):
    head_dim = HEAD_DIM
    heads_here = enc_query.shape[1] // head_dim
    cross_here = key_map.shape[1] // head_dim
    rows = enc_query.shape[0]
    tgt_rows = tgt_query.shape[0]
    query = enc_query.reshape(rows, heads_here, head_dim)
    own_key = enc_key.reshape(rows, heads_here, head_dim)
    own_value = enc_value.reshape(rows, heads_here, head_dim)
    own_mark = (doc_ids + 1).astype(jnp.bfloat16)
    arrived = {}
    for offset in (1, -1):
        arrived[offset] = passed_along((own_key, own_value, own_mark), "ctx", offset)
    left_key, left_value, left_mark = arrived[1]
    right_key, right_value, right_mark = arrived[-1]
    keys = jnp.concatenate([left_key, own_key, right_key], 0)
    values = jnp.concatenate([left_value, own_value, right_value], 0)
    marks = jnp.concatenate([left_mark, own_mark, right_mark], 0)
    enc_out = dense_attend(query, keys, values, own_mark, marks).astype(jnp.bfloat16)
    enc_flat = enc_out.reshape(rows, heads_here * head_dim)
    enc_full = lax.all_gather(enc_flat, "head", axis=1, tiled=True)
    key_sum = jnp.dot(
        enc_full,
        lax.all_gather(key_map, "ctx", axis=0, tiled=True),
        preferred_element_type=jnp.float32,
    )
    value_sum = jnp.dot(
        enc_full,
        lax.all_gather(value_map, "ctx", axis=0, tiled=True),
        preferred_element_type=jnp.float32,
    )
    memory_key = key_sum.astype(jnp.bfloat16).reshape(rows, cross_here, head_dim)
    memory_value = value_sum.astype(jnp.bfloat16).reshape(rows, cross_here, head_dim)
    target = tgt_query.reshape(tgt_rows, cross_here, head_dim)
    target_mark = own_mark.reshape(tgt_rows, rows // tgt_rows)[:, 0]
    near = {}
    for offset in (1, -1):
        near[offset] = passed_along((memory_key, memory_value, own_mark), "ctx", offset)
    keys = jnp.concatenate([near[1][0], memory_key, near[-1][0]], 0)
    values = jnp.concatenate([near[1][1], memory_value, near[-1][1]], 0)
    marks = jnp.concatenate([near[1][2], own_mark, near[-1][2]], 0)
    cross_out = dense_attend(target, keys, values, target_mark, marks)
    return cross_out.astype(jnp.bfloat16).reshape(tgt_rows, cross_here * head_dim)


def solution(mesh):
    in_specs = (
        P(("dp", "ctx"), "head"),
        P(("dp", "ctx"), "head"),
        P(("dp", "ctx"), "head"),
        P(("dp", "ctx")),
        P("ctx", "head"),
        P("ctx", "head"),
        P(("dp", "ctx"), "head"),
    )
    out_specs = P(("dp", "ctx"), "head")
    return jax.shard_map(
        on_device, mesh=mesh, in_specs=in_specs, out_specs=out_specs, check_vma=False
    )
```

profile of v0, /device:TPU:1, one launch (start us, length us, event | category | flops | bytes accessed | tf_op | source)
XLA Modules:
  0.0 251.3 jit_solution(5553337462665344755)
XLA Ops:
  6.5 1.3 copy.34
  8.1 4.6 %collective-permute-start.4 = (bf16[256,4,256]{2,0,1:T(8,128)(2,1)S(1)}, bf16[256,4,256]{2,0,1:T(8,128)(2,1)S(1)}, u32[]{:S(2)}, u32[]{:S(2)}) collective-permute-start(bf16[256,4,256]{2,0,1:T(8,128)(2,1)S(1)} %copy.35), channel_id=1, source_target_pairs={{0,4},{4,8},{8,12},{12,16},{16,20},{20,24},{24,28},{28,32},{32,36}... | collective-permute-start | bytes 1572872 | tf_op jit(solution)/shard_map/ppermute | solution.py:15
  12.6 5.5 %collective-permute-start.5 = (bf16[256,4,256]{2,0,1:T(8,128)(2,1)S(1)}, bf16[256,4,256]{2,0,1:T(8,128)(2,1)S(1)}, u32[]{:S(2)}, u32[]{:S(2)}) collective-permute-start(bf16[256,4,256]{2,0,1:T(8,128)(2,1)S(1)} %copy.35), channel_id=1, source_target_pairs={{4,0},{8,4},{12,8},{16,12},{20,16},{24,20},{28,24},{32,28},{36,32}... | collective-permute-start | bytes 1572872 | tf_op jit(solution)/shard_map/ppermute | solution.py:15
  18.1 0.7 add_convert_fusion
  18.8 1.9 collective-permute-start.2
  20.7 2.4 collective-permute-start.3
  23.1 1.2 copy.33
  24.4 3.2 %collective-permute-start = (bf16[256,4,256]{0,2,1:T(8,128)(2,1)S(1)}, bf16[256,4,256]{0,2,1:T(8,128)(2,1)S(1)}, u32[]{:S(2)}, u32[]{:S(2)}) collective-permute-start(bf16[256,4,256]{0,2,1:T(8,128)(2,1)S(1)} %bitcast.60), channel_id=1, source_target_pairs={{0,4},{4,8},{8,12},{12,16},{16,20},{20,24},{24,28},{28,32},{32,36}... | collective-permute-start | bytes 1572872 | tf_op jit(solution)/shard_map/ppermute | solution.py:15
  27.6 1.9 collective-permute-start.1
  30.4 0.7 fusion
  31.1 2.6 %collective-permute-done = bf16[256,4,256]{0,2,1:T(8,128)(2,1)S(1)} collective-permute-done((bf16[256,4,256]{0,2,1:T(8,128)(2,1)S(1)}, bf16[256,4,256]{0,2,1:T(8,128)(2,1)S(1)}, u32[]{:S(2)}, u32[]{:S(2)}) %collective-permute-start) | collective-permute-done | bytes 524320 | tf_op jit(solution)/shard_map/ppermute | solution.py:15
  33.7 8.0 %collective-permute-done.1 = bf16[256,4,256]{0,2,1:T(8,128)(2,1)S(1)} collective-permute-done((bf16[256,4,256]{0,2,1:T(8,128)(2,1)S(1)}, bf16[256,4,256]{0,2,1:T(8,128)(2,1)S(1)}, u32[]{:S(2)}, u32[]{:S(2)}) %collective-permute-start.1) | collective-permute-done | bytes 524320 | tf_op jit(solution)/shard_map/ppermute | solution.py:15
  41.7 1.9 divide_convert_fusion
  43.6 0.7 all-gather.8.cloned.1.call-update
  45.4 40.4 %all-gather.4.cloned.1.call-done = bf16[256,4096]{0,1:T(8,128)(2,1)} async-done(((bf16[256,1024]{0,1:T(8,128)(2,1)}), bf16[256,4096]{0,1:T(8,128)(2,1)}) %all-gather.4.cloned.1.call-update) | async-done | bytes 2097168 | tf_op jit(solution)/shard_map/all_gather | solution.py:62
  85.8 72.5 %all-gather.8.cloned.1.call-done = bf16[4096,512]{1,0:T(8,128)(2,1)} async-done(((bf16[128,512]{1,0:T(8,128)(2,1)}), bf16[4096,512]{1,0:T(8,128)(2,1)}) %all-gather.8.cloned.1.call-update) | async-done | bytes 4194320 | tf_op jit(solution)/shard_map/all_gather | solution.py:65
  158.3 4.1 %convolution_convert_fusion = bf16[256,512]{1,0:T(8,128)(2,1)S(1)} fusion(bf16[256,4096]{0,1:T(8,128)(2,1)} %all-gather.4.cloned.1.call-done, bf16[4096,512]{1,0:T(8,128)(2,1)} %all-gather.8.cloned.1.call-done), kind=kOutput, calls=%fused_computation.22 | convolution fusion | flops 1073872896 | bytes 6553600 | tf_op jit(solution)/shard_map/dot_general | solution.py:63
  162.4 2.9 %collective-permute-start.8 = (bf16[256,2,256]{2,0,1:T(8,128)(2,1)S(1)}, bf16[256,2,256]{2,0,1:T(8,128)(2,1)S(1)}, u32[]{:S(2)}, u32[]{:S(2)}) collective-permute-start(bf16[256,2,256]{2,0,1:T(8,128)(2,1)S(1)} %bitcast.64), channel_id=1, source_target_pairs={{0,4},{4,8},{8,12},{12,16},{16,20},{20,24},{24,28},{28,32},{32,36}... | collective-permute-start | bytes 786440 | tf_op jit(solution)/shard_map/ppermute | solution.py:15
  165.3 1.9 collective-permute-start.9
  167.2 62.5 %all-gather.6.cloned.1.call-done = bf16[4096,512]{1,0:T(8,128)(2,1)} async-done(((bf16[128,512]{1,0:T(8,128)(2,1)}), bf16[4096,512]{1,0:T(8,128)(2,1)}) %all-gather.6.cloned.1.call-update) | async-done | bytes 4194320 | tf_op jit(solution)/shard_map/all_gather | solution.py:70
  229.8 3.4 %convolution_convert_fusion.1 = bf16[256,512]{1,0:T(8,128)(2,1)S(1)} fusion(bf16[256,4096]{0,1:T(8,128)(2,1)S(1)} %copy-done, bf16[4096,512]{1,0:T(8,128)(2,1)} %all-gather.6.cloned.1.call-done), kind=kOutput, calls=%fused_computation.23 | convolution fusion | flops 1073872896 | bytes 6553600 | tf_op jit(solution)/shard_map/dot_general | solution.py:68
  233.3 2.8 %collective-permute-start.6 = (bf16[256,2,256]{2,0,1:T(8,128)(2,1)S(1)}, bf16[256,2,256]{2,0,1:T(8,128)(2,1)S(1)}, u32[]{:S(2)}, u32[]{:S(2)}) collective-permute-start(bf16[256,2,256]{2,0,1:T(8,128)(2,1)S(1)} %bitcast.67), channel_id=1, source_target_pairs={{0,4},{4,8},{8,12},{12,16},{16,20},{20,24},{24,28},{28,32},{32,36}... | collective-permute-start | bytes 786440 | tf_op jit(solution)/shard_map/ppermute | solution.py:15
  236.1 1.9 collective-permute-start.7
  239.3 4.4 %collective-permute-done.7 = bf16[256,2,256]{2,0,1:T(8,128)(2,1)S(1)} collective-permute-done((bf16[256,2,256]{2,0,1:T(8,128)(2,1)S(1)}, bf16[256,2,256]{2,0,1:T(8,128)(2,1)S(1)}, u32[]{:S(2)}, u32[]{:S(2)}) %collective-permute-start.7) | collective-permute-done | bytes 262176 | tf_op jit(solution)/shard_map/ppermute | solution.py:15
  (31 shorter events, 4.6 us)
Async XLA Ops:
  6.5 23.2 %copy-start.1 = (bf16[256,1024]{1,0:T(8,128)(2,1)S(1)}, bf16[256,1024]{1,0:T(8,128)(2,1)}, u32[]{:S(2)}) copy-start(bf16[256,1024]{1,0:T(8,128)(2,1)} %param.7) | copy-start | bytes 1572868
  6.5 79.3 %all-gather.4.cloned.1.call-start = ((), (), s32[]{:S(2)}) async-start(), calls=%async_computation | async-start | bytes 2621440 | tf_op jit(solution)/shard_map/all_gather | solution.py:62
  8.1 21.7 %collective-permute-start.4 = (bf16[256,4,256]{2,0,1:T(8,128)(2,1)S(1)}, bf16[256,4,256]{2,0,1:T(8,128)(2,1)S(1)}, u32[]{:S(2)}, u32[]{:S(2)}) collective-permute-start(bf16[256,4,256]{2,0,1:T(8,128)(2,1)S(1)} %copy.35), channel_id=1, source_target_pairs={{0,4},{4,8},{8,12},{12,16},{16,20},{20,24},{24,28},{28,32},{32,36}... | collective-permute-start | bytes 1572872 | tf_op jit(solution)/shard_map/ppermute | solution.py:15
  12.6 17.1 %collective-permute-start.5 = (bf16[256,4,256]{2,0,1:T(8,128)(2,1)S(1)}, bf16[256,4,256]{2,0,1:T(8,128)(2,1)S(1)}, u32[]{:S(2)}, u32[]{:S(2)}) collective-permute-start(bf16[256,4,256]{2,0,1:T(8,128)(2,1)S(1)} %copy.35), channel_id=1, source_target_pairs={{4,0},{8,4},{12,8},{16,12},{20,16},{24,20},{28,24},{32,28},{36,32}... | collective-permute-start | bytes 1572872 | tf_op jit(solution)/shard_map/ppermute | solution.py:15
  18.8 8.7 %collective-permute-start.2 = (bf16[256]{0:T(256)(128)(2,1)S(1)}, bf16[256]{0:T(256)(128)(2,1)S(1)}, u32[]{:S(2)}, u32[]{:S(2)}) collective-permute-start(bf16[256]{0:T(256)(128)(2,1)S(1)} %add_convert_fusion), channel_id=1, source_target_pairs={{0,4},{4,8},{8,12},{12,16},{16,20},{20,24},{24,28},{28,32},{32,36}... | collective-permute-start | bytes 1544 | tf_op jit(solution)/shard_map/ppermute | solution.py:15
  20.7 8.8 %collective-permute-start.3 = (bf16[256]{0:T(256)(128)(2,1)S(1)}, bf16[256]{0:T(256)(128)(2,1)S(1)}, u32[]{:S(2)}, u32[]{:S(2)}) collective-permute-start(bf16[256]{0:T(256)(128)(2,1)S(1)} %add_convert_fusion), channel_id=1, source_target_pairs={{4,0},{8,4},{12,8},{16,12},{20,16},{24,20},{28,24},{32,28},{36,32}... | collective-permute-start | bytes 1544 | tf_op jit(solution)/shard_map/ppermute | solution.py:15
  24.4 9.3 %collective-permute-start = (bf16[256,4,256]{0,2,1:T(8,128)(2,1)S(1)}, bf16[256,4,256]{0,2,1:T(8,128)(2,1)S(1)}, u32[]{:S(2)}, u32[]{:S(2)}) collective-permute-start(bf16[256,4,256]{0,2,1:T(8,128)(2,1)S(1)} %bitcast.60), channel_id=1, source_target_pairs={{0,4},{4,8},{8,12},{12,16},{16,20},{20,24},{24,28},{28,32},{32,36}... | collective-permute-start | bytes 1572872 | tf_op jit(solution)/shard_map/ppermute | solution.py:15
  27.6 14.1 %collective-permute-start.1 = (bf16[256,4,256]{0,2,1:T(8,128)(2,1)S(1)}, bf16[256,4,256]{0,2,1:T(8,128)(2,1)S(1)}, u32[]{:S(2)}, u32[]{:S(2)}) collective-permute-start(bf16[256,4,256]{0,2,1:T(8,128)(2,1)S(1)} %bitcast.61), channel_id=1, source_target_pairs={{4,0},{8,4},{12,8},{16,12},{20,16},{24,20},{28,24},{32,28},{36,32}... | collective-permute-start | bytes 1572872 | tf_op jit(solution)/shard_map/ppermute | solution.py:15
  43.6 114.7 %all-gather.8.cloned.1.call-start = ((), (), s32[]{:S(2)}) async-start(), calls=%async_computation.2 | async-start | bytes 4325376 | tf_op jit(solution)/shard_map/all_gather | solution.py:65
  44.3 185.5 %all-gather.6.cloned.1.call-start = ((), (), s32[]{:S(2)}) async-start(), calls=%async_computation.1 | async-start | bytes 4325376 | tf_op jit(solution)/shard_map/all_gather | solution.py:70
  85.8 144.0 %copy-start = (bf16[256,4096]{0,1:T(8,128)(2,1)S(1)}, bf16[256,4096]{0,1:T(8,128)(2,1)}, u32[]{:S(2)}) copy-start(bf16[256,4096]{0,1:T(8,128)(2,1)} %all-gather.4.cloned.1.call-done) | copy-start | bytes 6291460
  162.4 75.6 %copy-start.2 = (bf16[64,512]{1,0:T(8,128)(2,1)S(1)}, bf16[64,512]{1,0:T(8,128)(2,1)}, u32[]{:S(2)}) copy-start(bf16[64,512]{1,0:T(8,128)(2,1)} %param.13) | copy-start | bytes 196612
  162.4 75.6 %collective-permute-start.8 = (bf16[256,2,256]{2,0,1:T(8,128)(2,1)S(1)}, bf16[256,2,256]{2,0,1:T(8,128)(2,1)S(1)}, u32[]{:S(2)}, u32[]{:S(2)}) collective-permute-start(bf16[256,2,256]{2,0,1:T(8,128)(2,1)S(1)} %bitcast.64), channel_id=1, source_target_pairs={{0,4},{4,8},{8,12},{12,16},{16,20},{20,24},{24,28},{28,32},{32,36}... | collective-permute-start | bytes 786440 | tf_op jit(solution)/shard_map/ppermute | solution.py:15
  165.3 72.7 %collective-permute-start.9 = (bf16[256,2,256]{2,0,1:T(8,128)(2,1)S(1)}, bf16[256,2,256]{2,0,1:T(8,128)(2,1)S(1)}, u32[]{:S(2)}, u32[]{:S(2)}) collective-permute-start(bf16[256,2,256]{2,0,1:T(8,128)(2,1)S(1)} %bitcast.65), channel_id=1, source_target_pairs={{4,0},{8,4},{12,8},{16,12},{20,16},{24,20},{28,24},{32,28},{36,32}... | collective-permute-start | bytes 786440 | tf_op jit(solution)/shard_map/ppermute | solution.py:15
  233.3 6.1 %collective-permute-start.6 = (bf16[256,2,256]{2,0,1:T(8,128)(2,1)S(1)}, bf16[256,2,256]{2,0,1:T(8,128)(2,1)S(1)}, u32[]{:S(2)}, u32[]{:S(2)}) collective-permute-start(bf16[256,2,256]{2,0,1:T(8,128)(2,1)S(1)} %bitcast.67), channel_id=1, source_target_pairs={{0,4},{4,8},{8,12},{12,16},{16,20},{20,24},{24,28},{28,32},{32,36}... | collective-permute-start | bytes 786440 | tf_op jit(solution)/shard_map/ppermute | solution.py:15
  236.1 7.7 %collective-permute-start.7 = (bf16[256,2,256]{2,0,1:T(8,128)(2,1)S(1)}, bf16[256,2,256]{2,0,1:T(8,128)(2,1)S(1)}, u32[]{:S(2)}, u32[]{:S(2)}) collective-permute-start(bf16[256,2,256]{2,0,1:T(8,128)(2,1)S(1)} %bitcast.68), channel_id=1, source_target_pairs={{4,0},{8,4},{12,8},{16,12},{20,16},{24,20},{28,24},{32,28},{36,32}... | collective-permute-start | bytes 786440 | tf_op jit(solution)/shard_map/ppermute | solution.py:15
Sparse Core Ops, SparseCore 0:
  43.7 42.0 all-gather.3
  87.9 70.2 all-gather.7
  160.4 69.3 all-gather.5
where the time goes:
time: 252 us; the launch traced here: 251 us
  waiting for transfers between devices  192 us (76%)
  starting transfers between devices  29.1 us (12%)
  between operations  13.3 us (5%)
  matrix products  10.9 us (4%)
  local copies, waits for them, and re-layouts  3.67 us (1%)
    all_gather x1, waiting for transfers between devices, on_device(): lax.all_gather(key_map, 'ctx', axis=0, tiled=True)  72.5 us
    all_gather x1, waiting for transfers between devices, on_device(): lax.all_gather(value_map, 'ctx', axis=0, tiled=True)  62.5 us
    all_gather x1, waiting for transfers between devices, on_device(): enc_full = lax.all_gather(enc_flat, 'head', axis=1, tiled=True)  40.4 us
    ppermute x10, starting transfers between devices, passed_along(): lax.ppermute(value, axis, [(source, source + steps) for source in range(l...  29 us
    ppermute x10, waiting for transfers between devices, passed_along(): lax.ppermute(value, axis, [(source, source + steps) for source in range(l...  15.6 us
  transfers between devices with their start and end apart: 13, of which 7 were waited for; matrix products, arithmetic and copies ran while one was open for 5% of the time, Pallas kernels for 0%

commit v1 on v0

v1 whole, which is shorter than its diff:
```python
import functools

import jax
import jax.numpy as jnp
from jax import lax
from jax.experimental import pallas as pl
from jax.experimental.pallas import tpu as pltpu
from jax.sharding import PartitionSpec as P

MESH = pl.DeviceIdType.MESH
HEAD_DIM = 256
NEG_FILL = -1e30
SCALE = HEAD_DIM ** (-0.5)
F32 = jnp.float32
BF16 = jnp.bfloat16


def nt(a, b):
    return lax.dot_general(a, b, (((1,), (1,)), ((), ())), preferred_element_type=F32)


def nn(a, b):
    return lax.dot_general(a, b, (((1,), (0,)), ((), ())), preferred_element_type=F32)


def column_of(row, count, step):
    n = row.shape[1]
    i = lax.broadcasted_iota(jnp.int32, (count, n), 0)
    j = lax.broadcasted_iota(jnp.int32, (count, n), 1)
    return jnp.sum(jnp.where(j == step * i, row, 0.0), axis=1, keepdims=True)


def kernel(
    sizes,
    q_hbm,
    k_hbm,
    v_hbm,
    docs_hbm,
    wk_hbm,
    wv_hbm,
    tq_hbm,
    out_ref,
    qv,
    kb,
    vb,
    docs,
    tq,
    wk,
    wv,
    enc,
    mem,
    part_out,
    part_in,
    local_sem,
    halo_s,
    halo_r,
    small_s,
    small_r,
    zs,
    zr,
    ys,
    yr,
    ss,
    sr,
    xs,
    xr,
    xfs,
    xfr,
    cs,
    cr,
):
    n_dp, n_ctx, n_x = sizes
    n_z = n_ctx // 4
    dp = lax.axis_index("dp")
    ctx = lax.axis_index("ctx")
    x = lax.axis_index("head")
    core = lax.rem(ctx, 2)
    yl = lax.rem(ctx // 2, 2)
    z = ctx // 4

    heads = k_hbm.shape[1] // HEAD_DIM
    rows = k_hbm.shape[0]
    tgts = tq_hbm.shape[0]
    crosses = wk_hbm.shape[1] // HEAD_DIM
    wrows = wk_hbm.shape[0]

    left = (dp, lax.rem(ctx + n_ctx - 1, n_ctx), x)
    right = (dp, lax.rem(ctx + 1, n_ctx), x)
    zp = (dp, lax.rem(ctx + 4, n_ctx), x)
    zm = (dp, lax.rem(ctx + n_ctx - 4, n_ctx), x)
    pair = (dp, ctx + 2 - 4 * yl, x)
    across = (lax.rem(dp + 2 * yl - 1 + n_dp, n_dp), ctx + 2 - 4 * yl, x)
    sib = (dp, ctx + 1 - 2 * core, x)
    xp = (dp, ctx, lax.rem(x + 1, n_x))
    xm = (dp, ctx, lax.rem(x + n_x - 1, n_x))

    def remote(src, dst, send, recv, device):
        return pltpu.make_async_remote_copy(
            src_ref=src, dst_ref=dst, send_sem=send, recv_sem=recv,
            device_id=device, device_id_type=MESH,
        )

    barrier = pltpu.get_barrier_semaphore()
    partners = (left, right, zp, zm, pair, across, sib, xp, xm)
    for device in partners:
        pl.semaphore_signal(barrier, inc=1, device_id=device, device_id_type=MESH)

    locals_ = [
        pltpu.make_async_copy(docs_hbm, docs.at[1], local_sem.at[0]),
        pltpu.make_async_copy(q_hbm, qv, local_sem.at[1]),
        pltpu.make_async_copy(tq_hbm, tq.at[1], local_sem.at[2]),
    ]
    for h in range(heads):
        cols = pl.ds(h * HEAD_DIM, HEAD_DIM)
        locals_.append(pltpu.make_async_copy(k_hbm.at[:, cols], kb.at[1, h], local_sem.at[3 + 2 * h]))
        locals_.append(pltpu.make_async_copy(v_hbm.at[:, cols], vb.at[1, h], local_sem.at[4 + 2 * h]))

    def shard(zz, yy, cc):
        return pl.ds(pl.multiple_of((zz * 4 + yy * 2 + cc) * wrows, wrows), wrows)

    own_rows = shard(z, yl, core)
    base = 3 + 2 * heads
    locals_.append(pltpu.make_async_copy(wk_hbm, wk.at[own_rows], local_sem.at[base]))
    locals_.append(pltpu.make_async_copy(wv_hbm, wv.at[own_rows], local_sem.at[base + 1]))
    for copy in locals_:
        copy.start()

    pl.semaphore_wait(barrier, len(partners))

    sends = []

    def go(copy):
        copy.start()
        sends.append(copy)
        return copy

    sides = ((left, 2), (right, 0))
    halo = {}
    small = {}
    for side, (device, slot) in enumerate(sides):
        small[side, 0] = go(remote(docs_hbm, docs.at[slot], small_s.at[side, 0], small_r.at[side, 0], device))

    def start_halo(h):
        cols = pl.ds(h * HEAD_DIM, HEAD_DIM)
        for side, (device, slot) in enumerate(sides):
            halo[side, 0, h] = go(remote(
                k_hbm.at[:, cols], kb.at[slot, h], halo_s.at[side, 0, h], halo_r.at[side, 0, h], device))
            halo[side, 1, h] = go(remote(
                v_hbm.at[:, cols], vb.at[slot, h], halo_s.at[side, 1, h], halo_r.at[side, 1, h], device))

    w_of = (wk, wv)
    w_hbm = (wk_hbm, wv_hbm)
    zmove, ymove, smove = {}, {}, {}

    def zz_of(d):
        return lax.rem(z + d + n_z, n_z)

    def send_z(direction, step, kv, src):
        d = (1 - step) if direction == 0 else (step - 1)
        at = shard(zz_of(d), yl, core)
        device = zp if direction == 0 else zm
        if src is None:
            src = w_of[kv].at[at]
        zmove[direction, step, kv] = go(remote(
            src, w_of[kv].at[at], zs.at[direction, step - 1, kv], zr.at[direction, step - 1, kv], device))

    def send_y(d, kv, src):
        at = shard(zz_of(d), yl, core)
        far = (abs(d) == 3 and kv == 0) or abs(d) == 4
        device = pair if far else across
        if src is None:
            src = w_of[kv].at[at]
        ymove[d, kv] = go(remote(
            src, w_of[kv].at[at], ys.at[d + 3, kv], yr.at[d + 3, kv], device))

    def send_sib(parity, d, kv, src):
        yy = yl if parity == 0 else 1 - yl
        at = shard(zz_of(d), yy, core)
        if src is None:
            src = w_of[kv].at[at]
        smove[parity, d, kv] = go(remote(
            src, w_of[kv].at[at], ss.at[parity, d + 3, kv], sr.at[parity, d + 3, kv], sib))

    half = n_z // 2

    def arrive_z(direction, step, kv):
        zmove[direction, step, kv].wait_recv()
        d = -step if direction == 0 else step
        if step == half:
            d = half
        if step + 1 < half or (step + 1 == half and kv == direction):
            send_z(direction, step + 1, kv, None)
        send_y(d, kv, None)
        send_sib(0, d, kv, None)

    def arrive_y(d, kv):
        ymove[d, kv].wait_recv()
        send_sib(1, d, kv, None)

    def ring_step(step):
        for kv in range(2):
            for direction in range(2):
                if step < half or kv == direction:
                    arrive_z(direction, step, kv)

    start_halo(0)
    for kv in range(2):
        send_z(0, 1, kv, w_hbm[kv])
        send_z(1, 1, kv, w_hbm[kv])
        send_y(0, kv, w_hbm[kv])
    for h in range(1, heads):
        start_halo(h)
    for kv in range(2):
        send_sib(0, 0, kv, w_hbm[kv])
    for side, (device, slot) in enumerate(sides):
        small[side, 1] = go(remote(tq_hbm, tq.at[slot], small_s.at[side, 1], small_r.at[side, 1], device))

    for copy in locals_:
        copy.wait()
    for side in range(2):
        small[side, 0].wait_recv()

    marks = [docs[slot, 0:1, :] for slot in range(3)]
    own_col = column_of(marks[1], rows, 1)

    xmove, xfwd = {}, {}

    def attend(h):
        for side in range(2):
            for kv in range(2):
                halo[side, kv, h].wait_recv()
        query = qv[:, h * HEAD_DIM:(h + 1) * HEAD_DIM]
        scores = []
        for slot in range(3):
            raw = nt(query, kb[slot, h]) * SCALE
            scores.append(jnp.where(own_col == marks[slot], raw, NEG_FILL))
        top = jnp.max(jnp.maximum(jnp.maximum(scores[0], scores[1]), scores[2]), axis=1, keepdims=True)
        weights = [jnp.exp(s - top) for s in scores]
        total = jnp.sum(weights[0] + weights[1] + weights[2], axis=1, keepdims=True)
        summed = sum(nn(weights[slot].astype(BF16), vb[slot, h]) for slot in range(3))
        at = pl.ds(pl.multiple_of((x * heads + h) * HEAD_DIM, HEAD_DIM), HEAD_DIM)
        enc[:, at] = (summed / total).astype(BF16)
        for side, device in enumerate((xp, xm)):
            xmove[side, h] = go(remote(enc.at[:, at], enc.at[:, at], xs.at[side, h], xr.at[side, h], device))

    def hand_on(h):
        for side in range(2):
            xmove[side, h].wait_recv()
        side = h % 2
        source = lax.rem(x + n_x - 1, n_x) if side == 0 else lax.rem(x + 1, n_x)
        at = pl.ds(pl.multiple_of((source * heads + h) * HEAD_DIM, HEAD_DIM), HEAD_DIM)
        xfwd[h] = go(remote(enc.at[:, at], enc.at[:, at], xfs.at[h], xfr.at[h], (xp, xm)[side]))

    def come_y(*pieces):
        for d, kv in pieces:
            arrive_y(d, kv)

    ring_step(1)
    attend(0)
    come_y((0, 0), (0, 1))
    ring_step(2)
    hand_on(0)
    attend(1)
    come_y((-1, 0), (1, 0))
    ring_step(3)
    hand_on(1)
    attend(2)
    come_y((-1, 1), (1, 1))
    ring_step(4)
    hand_on(2)
    attend(3)
    come_y((-2, 0), (2, 0), (-2, 1), (2, 1))
    hand_on(3)
    come_y((-3, 1), (3, 1), (-3, 0), (3, 0), (4, 0), (4, 1))

    for h in range(heads):
        xfwd[h].wait_recv()
    for key in smove:
        smove[key].wait_recv()

    for kv in range(2):
        for n in range(crosses):
            cols = slice(n * HEAD_DIM, (n + 1) * HEAD_DIM)
            mem[kv, n] = nn(enc[...], w_of[kv][:, cols]).astype(BF16)

    for side in range(2):
        small[side, 1].wait_recv()
    lane = lax.broadcasted_iota(jnp.int32, (tgts, 128), 1)
    cmove = {}
    own = {}
    for n in range(crosses):
        cols = slice(n * HEAD_DIM, (n + 1) * HEAD_DIM)
        for slot in (0, 2, 1):
            col = column_of(marks[slot], tgts, rows // tgts)
            raw = nt(tq[slot, :, cols], mem[0, n]) * SCALE
            scores = jnp.where(col == marks[1], raw, NEG_FILL)
            top = jnp.max(scores, axis=1, keepdims=True)
            weights = jnp.exp(scores - top)
            total = jnp.sum(weights, axis=1, keepdims=True)
            summed = nn(weights.astype(BF16), mem[1, n])
            if slot == 1:
                own[n] = (top, total, summed)
                continue
            side = 0 if slot == 0 else 1
            part_out[side, n, :, 0:HEAD_DIM] = summed
            part_out[side, n, :, HEAD_DIM:] = jnp.where(lane == 0, top, total)
            cmove[side, n] = go(remote(
                part_out.at[side, n], part_in.at[1 - side, n], cs.at[side, n], cr.at[side, n], sides[side][0]))

    for n in range(crosses):
        top, total, summed = own[n]
        tops, totals, sums = [top], [total], [summed]
        for side in range(2):
            cmove[side, n].wait_recv()
            tops.append(part_in[1 - side, n, :, HEAD_DIM:HEAD_DIM + 1])
            totals.append(part_in[1 - side, n, :, HEAD_DIM + 1:HEAD_DIM + 2])
            sums.append(part_in[1 - side, n, :, 0:HEAD_DIM])
        most = jnp.maximum(jnp.maximum(tops[0], tops[1]), tops[2])
        factor = [jnp.exp(t - most) for t in tops]
        total = sum(f * t for f, t in zip(factor, totals))
        summed = sum(f * s for f, s in zip(factor, sums))
        out_ref[:, n * HEAD_DIM:(n + 1) * HEAD_DIM] = (summed / total).astype(BF16)

    for copy in sends:
        copy.wait_send()


def on_device(sizes, enc_query, enc_key, enc_value, doc_ids, key_map, value_map, tgt_query):
    rows, width = enc_key.shape
    heads = width // HEAD_DIM
    wrows, wcols = key_map.shape
    crosses = wcols // HEAD_DIM
    tgts = tgt_query.shape[0]
    n_z = sizes[1] // 4
    docs = jnp.broadcast_to(doc_ids.astype(F32)[None, :], (8, rows))
    dma = pltpu.SemaphoreType.DMA
    any_spec = pl.BlockSpec(memory_space=pl.ANY)
    return pl.pallas_call(
        functools.partial(kernel, sizes),
        out_shape=jax.ShapeDtypeStruct((tgts, wcols), BF16),
        in_specs=[any_spec] * 7,
        out_specs=pl.BlockSpec(memory_space=pltpu.VMEM),
        scratch_shapes=[
            pltpu.VMEM((rows, width), BF16),
            pltpu.VMEM((3, heads, rows, HEAD_DIM), BF16),
            pltpu.VMEM((3, heads, rows, HEAD_DIM), BF16),
            pltpu.VMEM((3, 8, rows), F32),
            pltpu.VMEM((3, tgts, wcols), BF16),
            pltpu.VMEM((wrows * sizes[1], wcols), BF16),
            pltpu.VMEM((wrows * sizes[1], wcols), BF16),
            pltpu.VMEM((rows, width * sizes[2]), BF16),
            pltpu.VMEM((2, crosses, rows, HEAD_DIM), BF16),
            pltpu.VMEM((2, crosses, tgts, HEAD_DIM + 128), F32),
            pltpu.VMEM((2, crosses, tgts, HEAD_DIM + 128), F32),
            dma((5 + 2 * heads,)),
            dma((2, 2, heads)),
            dma((2, 2, heads)),
            dma((2, 2)),
            dma((2, 2)),
            dma((2, n_z // 2, 2)),
            dma((2, n_z // 2, 2)),
            dma((n_z, 2)),
            dma((n_z, 2)),
            dma((2, n_z, 2)),
            dma((2, n_z, 2)),
            dma((2, heads)),
            dma((2, heads)),
            dma((heads,)),
            dma((heads,)),
            dma((2, crosses)),
            dma((2, crosses)),
        ],
        compiler_params=pltpu.CompilerParams(
            collective_id=0, has_side_effects=True, vmem_limit_bytes=60 * 1024 * 1024
        ),
    )(enc_query, enc_key, enc_value, docs, key_map, value_map, tgt_query)


def solution(mesh):
    sizes = (mesh.shape["dp"], mesh.shape["ctx"], mesh.shape["head"])
    in_specs = (
        P(("dp", "ctx"), "head"),
        P(("dp", "ctx"), "head"),
        P(("dp", "ctx"), "head"),
        P(("dp", "ctx")),
        P("ctx", "head"),
        P("ctx", "head"),
        P(("dp", "ctx"), "head"),
    )
    return jax.shard_map(
        functools.partial(on_device, sizes),
        mesh=mesh,
        in_specs=in_specs,
        out_specs=P(("dp", "ctx"), "head"),
        check_vma=False,
    )
```

time: 252 us -> 75 us (0.30)
  waiting for transfers between devices: 192 us -> 0 us
  Pallas kernels: 0 us -> 71.1 us
  starting transfers between devices: 29.1 us -> 0 us
  between operations: 13.3 us -> 0.01 us
  matrix products: 10.9 us -> 0 us
    all_gather x3 -> x0, waiting for transfers between devices: 175 us -> none  [the longest x1 72.5 us: on_device(): lax.all_gather(key_map, 'ctx', axis=0, tiled=True)]
    pallas_call x0 -> x1, Pallas kernels: none -> 71.1 us  [on_device(): pl.pallas_call(functools.partial(kernel, sizes), out_shape=jax.ShapeDtype...]
    ppermute x10 -> x0, starting transfers between devices: 29 us -> none  [passed_along(): lax.ppermute(value, axis, [(source, source + steps) for source in range(l...]
    ppermute x10 -> x0, waiting for transfers between devices: 15.6 us -> none  [passed_along(): lax.ppermute(value, axis, [(source, source + steps) for source in range(l...]
    dot_general x6 -> x0, matrix products: 10.9 us -> none  [the longest x1 4.08 us: on_device(): jnp.dot(enc_full, lax.all_gather(key_map, 'ctx', axis=0, tiled=True), pre...]
  transfers between devices with their start and end apart: 13 -> 0, of which waited for: 7 -> 0; matrix products, arithmetic and copies ran while one was open for 5% -> 0% of each run, Pallas kernels for 0% -> 0%
where the time goes in v1:
time: 75 us; the launch traced here: 73.8 us
  Pallas kernels  71.1 us (95%)
  local copies, waits for them, and re-layouts  2.08 us (3%)
    pallas_call x1, Pallas kernels, on_device(): pl.pallas_call(functools.partial(kernel, sizes), out_shape=jax.ShapeDtype...  71.1 us

profile of v1, /device:TPU:1, one launch (start us, length us, event | category | flops | bytes accessed | tf_op | source)
XLA Modules:
  0.0 73.8 jit_solution(15518906030986925613)
XLA Ops:
  0.0 0.7 convert_element_type.3
  0.7 0.6 broadcast_in_dim.2.docs_hbm
  1.3 71.1 %shard_map.73 = bf16[64,512]{1,0:T(8,128)(2,1)} custom-call(bf16[256,1024]{1,0:T(8,128)(2,1)} %q_hbm.1, bf16[256,1024]{1,0:T(8,128)(2,1)} %k_hbm.1, bf16[256,1024]{1,0:T(8,128)(2,1)} %v_hbm.1, f32[8,256]{1,0:T(8,128)} %broadcast_in_dim.2.docs_hbm, bf16[128,512]{1,0:T(8,128)(2,1)} %wk_hbm.1, bf16[128,512]{1,0:T(8,128)(2,1)} %wv_hbm.1, bf16[64,512]{1,0:T(8,128)(2,1)} %tq_hbm.1), custom_call_target="tpu_custom_call" | custom-call | tf_op jit(solution)/shard_map/pallas_call | solution.py:338
  72.4 1.5 %copy.9 = bf16[64,512]{1,0:T(8,128)(2,1)} copy(bf16[64,512]{1,0:T(8,128)(2,1)} %shard_map.73) | data formatting | bytes 131072

commit v2 on v1

v2 whole, which is shorter than its diff:
```python
import functools

import jax
import jax.numpy as jnp
from jax import lax
from jax.experimental import pallas as pl
from jax.experimental.pallas import tpu as pltpu
from jax.sharding import PartitionSpec as P

MESH = pl.DeviceIdType.MESH
HEAD_DIM = 256
NEG_FILL = -1e30
SCALE = HEAD_DIM ** (-0.5)
F32 = jnp.float32
BF16 = jnp.bfloat16


def nt(a, b):
    return lax.dot_general(a, b, (((1,), (1,)), ((), ())), preferred_element_type=F32)


def nn(a, b):
    return lax.dot_general(a, b, (((1,), (0,)), ((), ())), preferred_element_type=F32)


def column_of(row, count, step):
    n = row.shape[1]
    i = lax.broadcasted_iota(jnp.int32, (count, n), 0)
    j = lax.broadcasted_iota(jnp.int32, (count, n), 1)
    return jnp.sum(jnp.where(j == step * i, row, 0.0), axis=1, keepdims=True)


def kernel(
    sizes,
    q_hbm,
    k_hbm,
    v_hbm,
    docs_hbm,
    wk_hbm,
    wv_hbm,
    tq_hbm,
    out_ref,
    qv,
    kb,
    vb,
    docs,
    tq,
    w,
    enc,
    part_out,
    part_in,
    local_sem,
    own_w_sem,
    halo_s,
    halo_r,
    small_s,
    small_r,
    zs,
    zr,
    ys,
    yr,
    ss,
    sr,
    xs,
    xr,
    xfs,
    xfr,
    cs,
    cr,
):
    n_dp, n_ctx, n_x = sizes
    n_z = n_ctx // 4
    dp = lax.axis_index("dp")
    ctx = lax.axis_index("ctx")
    x = lax.axis_index("head")
    core = lax.rem(ctx, 2)
    yl = lax.rem(ctx // 2, 2)
    z = ctx // 4
    sign = 1 - 2 * yl

    heads = k_hbm.shape[1] // HEAD_DIM
    rows = k_hbm.shape[0]
    tgts = tq_hbm.shape[0]
    crosses = wk_hbm.shape[1] // HEAD_DIM
    wrows = wk_hbm.shape[0]

    left = (dp, lax.rem(ctx + n_ctx - 1, n_ctx), x)
    right = (dp, lax.rem(ctx + 1, n_ctx), x)
    long_to = (dp, lax.rem(ctx + n_ctx - 4 * sign, n_ctx), x)
    short_to = (dp, lax.rem(ctx + n_ctx + 4 * sign, n_ctx), x)
    pair = (dp, ctx + 2 - 4 * yl, x)
    across = (lax.rem(dp + 2 * yl - 1 + n_dp, n_dp), ctx + 2 - 4 * yl, x)
    sib = (dp, ctx + 1 - 2 * core, x)
    xp = (dp, ctx, lax.rem(x + 1, n_x))
    xm = (dp, ctx, lax.rem(x + n_x - 1, n_x))

    def remote(src, dst, send, recv, device):
        return pltpu.make_async_remote_copy(
            src_ref=src, dst_ref=dst, send_sem=send, recv_sem=recv,
            device_id=device, device_id_type=MESH,
        )

    barrier = pltpu.get_barrier_semaphore()
    partners = (left, right, long_to, short_to, pair, across, sib, xp, xm)
    for device in partners:
        pl.semaphore_signal(barrier, inc=1, device_id=device, device_id_type=MESH)

    def shard(e, yy):
        zz = lax.rem(z + sign * e + n_z, n_z)
        return pl.ds(pl.multiple_of((zz * 4 + yy * 2 + core) * wrows, wrows), wrows)

    own_w = []
    for n in range(crosses):
        cols = pl.ds(n * HEAD_DIM, HEAD_DIM)
        for kv, src in enumerate((wk_hbm, wv_hbm)):
            own_w.append(pltpu.make_async_copy(
                src.at[:, cols], w.at[n, shard(0, yl), pl.ds(kv * HEAD_DIM, HEAD_DIM)], own_w_sem.at[n, kv]))
    copies = [
        pltpu.make_async_copy(docs_hbm, docs.at[1], local_sem.at[0]),
        pltpu.make_async_copy(q_hbm, qv, local_sem.at[1]),
        pltpu.make_async_copy(tq_hbm, tq.at[2], local_sem.at[2]),
    ]
    for h in range(heads):
        cols = pl.ds(h * HEAD_DIM, HEAD_DIM)
        copies.append(pltpu.make_async_copy(k_hbm.at[:, cols], kb.at[1, h], local_sem.at[3 + 2 * h]))
        copies.append(pltpu.make_async_copy(v_hbm.at[:, cols], vb.at[1, h], local_sem.at[4 + 2 * h]))
    for copy in own_w + copies:
        copy.start()
    for copy in own_w:
        copy.wait()

    pl.semaphore_wait(barrier, len(partners))

    sends = []

    def go(copy):
        copy.start()
        sends.append(copy)
        return copy

    sides = ((left, 2), (right, 0))
    halo, small = {}, {}
    for side, (device, slot) in enumerate(sides):
        small[side, 0] = go(remote(docs_hbm, docs.at[slot], small_s.at[side, 0], small_r.at[side, 0], device))

    def start_halo(h):
        cols = pl.ds(h * HEAD_DIM, HEAD_DIM)
        for side, (device, slot) in enumerate(sides):
            halo[side, 0, h] = go(remote(
                k_hbm.at[:, cols], kb.at[slot, h], halo_s.at[side, 0, h], halo_r.at[side, 0, h], device))
            halo[side, 1, h] = go(remote(
                v_hbm.at[:, cols], vb.at[slot, h], halo_s.at[side, 1, h], halo_r.at[side, 1, h], device))

    far_y = ((3, 1), (4, 1), (5, 1), (6, 1))
    zmove, ymove, smove = {}, {}, {}

    def send_z(ring, step, n):
        e = step - 1 if ring == 0 else 1 - step
        at = w.at[n, shard(e, yl)]
        zmove[ring, step, n] = go(remote(
            at, at, zs.at[ring, step - 1, n], zr.at[ring, step - 1, n], long_to if ring == 0 else short_to))

    def send_y(e, n):
        at = w.at[n, shard(e, yl)]
        there = (n_z - e) % n_z
        ymove[there, n] = go(remote(
            at, at, ys.at[there, n], yr.at[there, n], pair if (e, n) in far_y else across))

    def send_sib(parity, e, n):
        at = w.at[n, shard(e, yl if parity == 0 else 1 - yl)]
        smove[parity, e, n] = go(remote(at, at, ss.at[parity, e, n], sr.at[parity, e, n], sib))

    def arrive(ring, step, n):
        zmove[ring, step, n].wait_recv()
        e = step if ring == 0 else n_z - step
        if ring == 0 and (step < 4 or (step == 4 and n == 0)):
            send_z(0, step + 1, n)
        if ring == 1 and (step < 2 or (step == 2 and n == 1)):
            send_z(1, step + 1, n)
        send_y(e, n)
        send_sib(0, e, n)

    def come_y(e, n):
        ymove[e, n].wait_recv()
        send_sib(1, e, n)

    for n in range(crosses):
        send_z(0, 1, n)
        send_z(1, 1, n)
        send_y(0, n)
    for h in range(heads):
        start_halo(h)
    for n in range(crosses):
        send_sib(0, 0, n)
    for side, (device, slot) in enumerate(sides):
        small[side, 1] = go(remote(tq_hbm, tq.at[1 - side], small_s.at[side, 1], small_r.at[side, 1], device))

    for copy in copies:
        copy.wait()
    for side in range(2):
        small[side, 0].wait_recv()

    marks = [docs[slot].astype(F32) for slot in range(3)]
    own_col = column_of(marks[1], rows, 1)
    tgt_col = [column_of(marks[slot], tgts, rows // tgts) for slot in range(3)]
    side_col = jnp.concatenate([tgt_col[0], tgt_col[2]], axis=0)

    xmove, xfwd = {}, {}

    def attend(h):
        for side in range(2):
            for kv in range(2):
                halo[side, kv, h].wait_recv()
        query = qv[:, h * HEAD_DIM:(h + 1) * HEAD_DIM]
        scores = []
        for slot in range(3):
            raw = nt(query, kb[slot, h]) * SCALE
            scores.append(jnp.where(own_col == marks[slot], raw, NEG_FILL))
        top = jnp.max(jnp.maximum(jnp.maximum(scores[0], scores[1]), scores[2]), axis=1, keepdims=True)
        weights = [jnp.exp(s - top) for s in scores]
        total = jnp.sum(weights[0] + weights[1] + weights[2], axis=1, keepdims=True)
        summed = sum(nn(weights[slot].astype(BF16), vb[slot, h]) for slot in range(3))
        at = pl.ds(pl.multiple_of((x * heads + h) * HEAD_DIM, HEAD_DIM), HEAD_DIM)
        enc[:, at] = (summed / total).astype(BF16)
        for side, device in enumerate((xp, xm)):
            xmove[side, h] = go(remote(enc.at[:, at], enc.at[:, at], xs.at[side, h], xr.at[side, h], device))

    def hand_on(h):
        for side in range(2):
            xmove[side, h].wait_recv()
        side = h % 2
        source = lax.rem(x + n_x - 1, n_x) if side == 0 else lax.rem(x + 1, n_x)
        at = pl.ds(pl.multiple_of((source * heads + h) * HEAD_DIM, HEAD_DIM), HEAD_DIM)
        xfwd[h] = go(remote(enc.at[:, at], enc.at[:, at], xfs.at[h], xfr.at[h], (xp, xm)[side]))

    arrive(0, 1, 0)
    arrive(0, 1, 1)
    come_y(0, 0)
    attend(0)
    arrive(1, 1, 0)
    arrive(0, 2, 0)
    come_y(0, 1)
    arrive(0, 2, 1)
    arrive(1, 1, 1)
    hand_on(0)
    attend(1)
    come_y(7, 0)
    come_y(7, 1)
    come_y(1, 0)
    arrive(0, 3, 0)
    arrive(0, 3, 1)
    arrive(1, 2, 0)
    hand_on(1)
    attend(2)
    come_y(6, 0)
    arrive(0, 4, 0)
    arrive(1, 2, 1)
    arrive(0, 4, 1)
    hand_on(2)
    attend(3)
    come_y(6, 1)
    come_y(1, 1)
    arrive(0, 5, 0)
    come_y(5, 0)
    arrive(1, 3, 1)
    come_y(2, 0)
    hand_on(3)
    come_y(4, 0)
    come_y(3, 0)

    for h in range(heads):
        xfwd[h].wait_recv()

    def maps(n):
        for parity in range(2):
            for e in range(n_z):
                smove[parity, e, n].wait_recv()
        both = nn(enc[...], w[n]).astype(BF16)
        return both[:, :HEAD_DIM], both[:, HEAD_DIM:]

    def partial_sums(query, col, memory):
        raw = nt(query, memory[0]) * SCALE
        scores = jnp.where(col == marks[1], raw, NEG_FILL)
        top = jnp.max(scores, axis=1, keepdims=True)
        weights = jnp.exp(scores - top)
        total = jnp.sum(weights, axis=1, keepdims=True)
        return top, total, nn(weights.astype(BF16), memory[1])

    lane = lax.broadcasted_iota(jnp.int32, (tgts, 128), 1)
    cmove = {}

    def give(n, memory):
        query = tq[0:2, :, n * HEAD_DIM:(n + 1) * HEAD_DIM].reshape(2 * tgts, HEAD_DIM)
        top, total, summed = partial_sums(query, side_col, memory)
        for side in range(2):
            at = slice(side * tgts, (side + 1) * tgts)
            part_out[side, n, :, 0:HEAD_DIM] = summed[at]
            part_out[side, n, :, HEAD_DIM:] = jnp.where(lane == 0, top[at], total[at])
            cmove[side, n] = go(remote(
                part_out.at[side, n], part_in.at[1 - side, n], cs.at[side, n], cr.at[side, n], sides[side][0]))

    def merge(n, own):
        tops, totals, sums = [own[0]], [own[1]], [own[2]]
        for side in range(2):
            cmove[side, n].wait_recv()
            tops.append(part_in[1 - side, n, :, HEAD_DIM:HEAD_DIM + 1])
            totals.append(part_in[1 - side, n, :, HEAD_DIM + 1:HEAD_DIM + 2])
            sums.append(part_in[1 - side, n, :, 0:HEAD_DIM])
        most = jnp.maximum(jnp.maximum(tops[0], tops[1]), tops[2])
        factor = [jnp.exp(t - most) for t in tops]
        total = sum(f * t for f, t in zip(factor, totals))
        summed = sum(f * s for f, s in zip(factor, sums))
        out_ref[:, n * HEAD_DIM:(n + 1) * HEAD_DIM] = summed / total

    for side in range(2):
        small[side, 1].wait_recv()
    own = {}
    for n in range(crosses):
        if n == 1:
            for e in (7, 6, 5, 2, 4, 3):
                if (e, 1) not in [key[1:] for key in smove if key[0] == 1]:
                    come_y(e, 1)
        memory = maps(n)
        give(n, memory)
        own[n] = partial_sums(tq[2, :, n * HEAD_DIM:(n + 1) * HEAD_DIM], tgt_col[1], memory)
    for n in range(crosses):
        merge(n, own[n])

    for copy in sends:
        copy.wait_send()


def on_device(sizes, enc_query, enc_key, enc_value, doc_ids, key_map, value_map, tgt_query):
    rows, width = enc_key.shape
    heads = width // HEAD_DIM
    wrows, wcols = key_map.shape
    crosses = wcols // HEAD_DIM
    tgts = tgt_query.shape[0]
    n_z = sizes[1] // 4
    docs = doc_ids.reshape(1, rows)
    dma = pltpu.SemaphoreType.DMA
    any_spec = pl.BlockSpec(memory_space=pl.ANY)
    out = pl.pallas_call(
        functools.partial(kernel, sizes),
        out_shape=jax.ShapeDtypeStruct((tgts, wcols), F32),
        in_specs=[any_spec] * 7,
        out_specs=pl.BlockSpec(memory_space=pltpu.VMEM),
        scratch_shapes=[
            pltpu.VMEM((rows, width), BF16),
            pltpu.VMEM((3, heads, rows, HEAD_DIM), BF16),
            pltpu.VMEM((3, heads, rows, HEAD_DIM), BF16),
            pltpu.VMEM((3, 1, rows), jnp.int32),
            pltpu.VMEM((3, tgts, wcols), BF16),
            pltpu.VMEM((crosses, wrows * sizes[1], 2 * HEAD_DIM), BF16),
            pltpu.VMEM((rows, width * sizes[2]), BF16),
            pltpu.VMEM((2, crosses, tgts, HEAD_DIM + 128), F32),
            pltpu.VMEM((2, crosses, tgts, HEAD_DIM + 128), F32),
            dma((3 + 2 * heads,)),
            dma((crosses, 2)),
            dma((2, 2, heads)),
            dma((2, 2, heads)),
            dma((2, 2)),
            dma((2, 2)),
            dma((2, 5, crosses)),
            dma((2, 5, crosses)),
            dma((n_z, crosses)),
            dma((n_z, crosses)),
            dma((2, n_z, crosses)),
            dma((2, n_z, crosses)),
            dma((2, heads)),
            dma((2, heads)),
            dma((heads,)),
            dma((heads,)),
            dma((2, crosses)),
            dma((2, crosses)),
        ],
        compiler_params=pltpu.CompilerParams(
            collective_id=0, has_side_effects=True, vmem_limit_bytes=60 * 1024 * 1024
        ),
    )(enc_query, enc_key, enc_value, docs, key_map, value_map, tgt_query)
    return out.astype(BF16)


def solution(mesh):
    sizes = (mesh.shape["dp"], mesh.shape["ctx"], mesh.shape["head"])
    in_specs = (
        P(("dp", "ctx"), "head"),
        P(("dp", "ctx"), "head"),
        P(("dp", "ctx"), "head"),
        P(("dp", "ctx")),
        P("ctx", "head"),
        P("ctx", "head"),
        P(("dp", "ctx"), "head"),
    )
    return jax.shard_map(
        functools.partial(on_device, sizes),
        mesh=mesh,
        in_specs=in_specs,
        out_specs=P(("dp", "ctx"), "head"),
        check_vma=False,
    )
```

time: 75 us -> 65.7 us (0.88)
  the two profiles are of different devices: /device:TPU:1 before, /device:TPU:54 now
where the time goes in v2:
time: 65.7 us; the launch traced here: 65.6 us
  Pallas kernels  64 us (97%)
  other arithmetic  1.54 us (2%)
    pallas_call x1, Pallas kernels, on_device(): pl.pallas_call(functools.partial(kernel, sizes), out_shape=jax.ShapeDtype...  64 us
    convert_element_type x1, other arithmetic, on_device(): return out.astype(BF16)  1.54 us

profile of v2, /device:TPU:54, one launch (start us, length us, event | category | flops | bytes accessed | tf_op | source)
XLA Modules:
  0.0 65.6 jit_solution(4189679990711415273)
XLA Ops:
  0.0 64.0 %shard_map.73 = f32[64,512]{1,0:T(8,128)} custom-call(bf16[256,1024]{1,0:T(8,128)(2,1)} %q_hbm.1, bf16[256,1024]{1,0:T(8,128)(2,1)} %k_hbm.1, bf16[256,1024]{1,0:T(8,128)(2,1)} %v_hbm.1, s32[1,256]{1,0:T(1,128)} %bitcast.1, bf16[128,512]{1,0:T(8,128)(2,1)} %wk_hbm.1, bf16[128,512]{1,0:T(8,128)(2,1)} %wv_hbm.1, bf16[64,512]{1,0:T(8,128)(2,1)} %tq_hbm.1), custom_call_target="tpu_custom_call" | custom-call | tf_op jit(solution)/shard_map/pallas_call | solution.py:343
  64.0 1.5 %convert_element_type.3 = bf16[64,512]{1,0:T(8,128)(2,1)} convert(f32[64,512]{1,0:T(8,128)} %shard_map.73) | non-fusion elementwise | flops 32768 | bytes 196608 | tf_op jit(solution)/shard_map/convert_element_type | solution.py:381

commit v3 on v2

--- a/solution.py
+++ b/solution.py
@@ -67,6 +67,8 @@
     xfr,
     cs,
     cr,
+    os_,
+    or_,
 ):
     n_dp, n_ctx, n_x = sizes
     n_z = n_ctx // 4
@@ -126,9 +128,6 @@
         copies.append(pltpu.make_async_copy(v_hbm.at[:, cols], vb.at[1, h], local_sem.at[4 + 2 * h]))
     for copy in own_w + copies:
         copy.start()
-    for copy in own_w:
-        copy.wait()
-
     pl.semaphore_wait(barrier, len(partners))
 
     sends = []
@@ -151,8 +150,9 @@
             halo[side, 1, h] = go(remote(
                 v_hbm.at[:, cols], vb.at[slot, h], halo_s.at[side, 1, h], halo_r.at[side, 1, h], device))
 
-    far_y = ((3, 1), (4, 1), (5, 1), (6, 1))
-    zmove, ymove, smove = {}, {}, {}
+    far_y = ((4, 0), (5, 0), (5, 1))
+    by_ring = ((6, 0), (6, 1), (4, 1))
+    zmove, ymove, smove, omove = {}, {}, {}, {}
 
     def send_z(ring, step, n):
         e = step - 1 if ring == 0 else 1 - step
@@ -161,6 +161,8 @@
             at, at, zs.at[ring, step - 1, n], zr.at[ring, step - 1, n], long_to if ring == 0 else short_to))
 
     def send_y(e, n):
+        if (e, n) in by_ring:
+            return
         at = w.at[n, shard(e, yl)]
         there = (n_z - e) % n_z
         ymove[there, n] = go(remote(
@@ -180,15 +182,27 @@
         send_y(e, n)
         send_sib(0, e, n)
 
+    def send_o(ring, n):
+        at = w.at[n, shard(1 if ring == 0 else 5, 1 - yl)]
+        omove[ring, n] = go(remote(
+            at, at, os_.at[ring, n], or_.at[ring, n], long_to if ring == 0 else short_to))
+
+    def come_o(ring, n):
+        omove[ring, n].wait_recv()
+        send_sib(1, 2 if ring == 0 else 4, n)
+
     def come_y(e, n):
         ymove[e, n].wait_recv()
         send_sib(1, e, n)
 
+    start_halo(0)
+    for copy in own_w:
+        copy.wait()
     for n in range(crosses):
         send_z(0, 1, n)
         send_z(1, 1, n)
         send_y(0, n)
-    for h in range(heads):
+    for h in range(1, heads):
         start_halo(h)
     for n in range(crosses):
         send_sib(0, 0, n)
@@ -206,6 +220,9 @@
     side_col = jnp.concatenate([tgt_col[0], tgt_col[2]], axis=0)
 
     xmove, xfwd = {}, {}
+
+    def half_rows(half):
+        return pl.ds(half * (rows // 2), rows // 2)
 
     def attend(h):
         for side in range(2):
@@ -222,54 +239,64 @@
         summed = sum(nn(weights[slot].astype(BF16), vb[slot, h]) for slot in range(3))
         at = pl.ds(pl.multiple_of((x * heads + h) * HEAD_DIM, HEAD_DIM), HEAD_DIM)
         enc[:, at] = (summed / total).astype(BF16)
+        for part in range(2):
+            for side, device in enumerate((xp, xm)):
+                piece = enc.at[half_rows(part if side == 0 else 1 - part), at]
+                xmove[side, h, part] = go(remote(piece, piece, xs.at[side, h, part], xr.at[side, h, part], device))
+
+    def hand_on(h):
         for side, device in enumerate((xp, xm)):
-            xmove[side, h] = go(remote(enc.at[:, at], enc.at[:, at], xs.at[side, h], xr.at[side, h], device))
-
-    def hand_on(h):
-        for side in range(2):
-            xmove[side, h].wait_recv()
-        side = h % 2
-        source = lax.rem(x + n_x - 1, n_x) if side == 0 else lax.rem(x + 1, n_x)
-        at = pl.ds(pl.multiple_of((source * heads + h) * HEAD_DIM, HEAD_DIM), HEAD_DIM)
-        xfwd[h] = go(remote(enc.at[:, at], enc.at[:, at], xfs.at[h], xfr.at[h], (xp, xm)[side]))
+            xmove[side, h, 0].wait_recv()
+            source = lax.rem(x + n_x - 1, n_x) if side == 0 else lax.rem(x + 1, n_x)
+            at = pl.ds(pl.multiple_of((source * heads + h) * HEAD_DIM, HEAD_DIM), HEAD_DIM)
+            piece = enc.at[half_rows(side), at]
+            xfwd[side, h] = go(remote(piece, piece, xfs.at[side, h], xfr.at[side, h], device))
 
     arrive(0, 1, 0)
+    come_y(0, 0)
     arrive(0, 1, 1)
-    come_y(0, 0)
     attend(0)
+    come_y(0, 1)
     arrive(1, 1, 0)
     arrive(0, 2, 0)
-    come_y(0, 1)
+    come_y(7, 0)
     arrive(0, 2, 1)
     arrive(1, 1, 1)
+    attend(1)
     hand_on(0)
-    attend(1)
-    come_y(7, 0)
     come_y(7, 1)
-    come_y(1, 0)
     arrive(0, 3, 0)
     arrive(0, 3, 1)
     arrive(1, 2, 0)
+    attend(2)
     hand_on(1)
-    attend(2)
+    come_y(1, 0)
     come_y(6, 0)
     arrive(0, 4, 0)
+    send_o(0, 0)
+    arrive(0, 4, 1)
     arrive(1, 2, 1)
-    arrive(0, 4, 1)
+    attend(3)
     hand_on(2)
-    attend(3)
     come_y(6, 1)
     come_y(1, 1)
+    send_o(0, 1)
     arrive(0, 5, 0)
+    come_y(4, 0)
     come_y(5, 0)
+    come_y(5, 1)
+    send_o(1, 1)
     arrive(1, 3, 1)
-    come_y(2, 0)
     hand_on(3)
-    come_y(4, 0)
+    come_o(0, 0)
     come_y(3, 0)
+    come_o(0, 1)
+    come_o(1, 1)
 
     for h in range(heads):
-        xfwd[h].wait_recv()
+        for side in range(2):
+            xmove[side, h, 1].wait_recv()
+            xfwd[side, h].wait_recv()
 
     def maps(n):
         for parity in range(2):
@@ -286,16 +313,21 @@
         total = jnp.sum(weights, axis=1, keepdims=True)
         return top, total, nn(weights.astype(BF16), memory[1])
 
-    lane = lax.broadcasted_iota(jnp.int32, (tgts, 128), 1)
+    diagonal = lax.broadcasted_iota(jnp.int32, (tgts, HEAD_DIM), 0) == lax.broadcasted_iota(
+        jnp.int32, (tgts, HEAD_DIM), 1)
+    first_row = lax.broadcasted_iota(jnp.int32, (8, HEAD_DIM), 0) == 0
     cmove = {}
+
+    def row_of(column):
+        return jnp.sum(jnp.where(diagonal, column, 0.0), axis=0, keepdims=True)
 
     def give(n, memory):
         query = tq[0:2, :, n * HEAD_DIM:(n + 1) * HEAD_DIM].reshape(2 * tgts, HEAD_DIM)
         top, total, summed = partial_sums(query, side_col, memory)
         for side in range(2):
             at = slice(side * tgts, (side + 1) * tgts)
-            part_out[side, n, :, 0:HEAD_DIM] = summed[at]
-            part_out[side, n, :, HEAD_DIM:] = jnp.where(lane == 0, top[at], total[at])
+            part_out[side, n, 0:tgts] = summed[at]
+            part_out[side, n, tgts:] = jnp.where(first_row, row_of(top[at]), row_of(total[at]))
             cmove[side, n] = go(remote(
                 part_out.at[side, n], part_in.at[1 - side, n], cs.at[side, n], cr.at[side, n], sides[side][0]))
 
@@ -303,9 +335,9 @@
         tops, totals, sums = [own[0]], [own[1]], [own[2]]
         for side in range(2):
             cmove[side, n].wait_recv()
-            tops.append(part_in[1 - side, n, :, HEAD_DIM:HEAD_DIM + 1])
-            totals.append(part_in[1 - side, n, :, HEAD_DIM + 1:HEAD_DIM + 2])
-            sums.append(part_in[1 - side, n, :, 0:HEAD_DIM])
+            tops.append(column_of(part_in[1 - side, n, tgts:tgts + 1], tgts, 1))
+            totals.append(column_of(part_in[1 - side, n, tgts + 1:tgts + 2], tgts, 1))
+            sums.append(part_in[1 - side, n, 0:tgts])
         most = jnp.maximum(jnp.maximum(tops[0], tops[1]), tops[2])
         factor = [jnp.exp(t - most) for t in tops]
         total = sum(f * t for f, t in zip(factor, totals))
@@ -314,15 +346,15 @@
 
     for side in range(2):
         small[side, 1].wait_recv()
-    own = {}
+    memory = {}
     for n in range(crosses):
         if n == 1:
-            for e in (7, 6, 5, 2, 4, 3):
-                if (e, 1) not in [key[1:] for key in smove if key[0] == 1]:
-                    come_y(e, 1)
-        memory = maps(n)
-        give(n, memory)
-        own[n] = partial_sums(tq[2, :, n * HEAD_DIM:(n + 1) * HEAD_DIM], tgt_col[1], memory)
+            come_y(3, 1)
+        memory[n] = maps(n)
+        give(n, memory[n])
+    own = [
+        partial_sums(tq[2, :, n * HEAD_DIM:(n + 1) * HEAD_DIM], tgt_col[1], memory[n]) for n in range(crosses)
+    ]
     for n in range(crosses):
         merge(n, own[n])
 
@@ -353,8 +385,8 @@
             pltpu.VMEM((3, tgts, wcols), BF16),
             pltpu.VMEM((crosses, wrows * sizes[1], 2 * HEAD_DIM), BF16),
             pltpu.VMEM((rows, width * sizes[2]), BF16),
-            pltpu.VMEM((2, crosses, tgts, HEAD_DIM + 128), F32),
-            pltpu.VMEM((2, crosses, tgts, HEAD_DIM + 128), F32),
+            pltpu.VMEM((2, crosses, tgts + 8, HEAD_DIM), F32),
+            pltpu.VMEM((2, crosses, tgts + 8, HEAD_DIM), F32),
             dma((3 + 2 * heads,)),
             dma((crosses, 2)),
             dma((2, 2, heads)),
@@ -367,10 +399,12 @@
             dma((n_z, crosses)),
             dma((2, n_z, crosses)),
             dma((2, n_z, crosses)),
+            dma((2, heads, 2)),
+            dma((2, heads, 2)),
             dma((2, heads)),
             dma((2, heads)),
-            dma((heads,)),
-            dma((heads,)),
+            dma((2, crosses)),
+            dma((2, crosses)),
             dma((2, crosses)),
             dma((2, crosses)),
         ],

time: 65.7 us -> 60.1 us (0.915)
  the two profiles are of different devices: /device:TPU:54 before, /device:TPU:1 now
where the time goes in v3:
time: 60.1 us; the launch traced here: 59.1 us
  Pallas kernels  57.5 us (96%)
  other arithmetic  1.54 us (3%)
    pallas_call x1, Pallas kernels, on_device(): pl.pallas_call(functools.partial(kernel, sizes), out_shape=jax.ShapeDtype...  57.5 us
    convert_element_type x1, other arithmetic, on_device(): return out.astype(BF16)  1.54 us

profile of v3, /device:TPU:1, one launch (start us, length us, event | category | flops | bytes accessed | tf_op | source)
XLA Modules:
  0.0 59.1 jit_solution(17846509435144566371)
XLA Ops:
  0.0 57.5 %shard_map.73 = f32[64,512]{1,0:T(8,128)} custom-call(bf16[256,1024]{1,0:T(8,128)(2,1)} %q_hbm.1, bf16[256,1024]{1,0:T(8,128)(2,1)} %k_hbm.1, bf16[256,1024]{1,0:T(8,128)(2,1)} %v_hbm.1, s32[1,256]{1,0:T(1,128)} %bitcast.1, bf16[128,512]{1,0:T(8,128)(2,1)} %wk_hbm.1, bf16[128,512]{1,0:T(8,128)(2,1)} %wv_hbm.1, bf16[64,512]{1,0:T(8,128)(2,1)} %tq_hbm.1), custom_call_target="tpu_custom_call" | custom-call | tf_op jit(solution)/shard_map/pallas_call | solution.py:375
  57.5 1.5 %convert_element_type.3 = bf16[64,512]{1,0:T(8,128)(2,1)} convert(f32[64,512]{1,0:T(8,128)} %shard_map.73) | non-fusion elementwise | flops 32768 | bytes 196608 | tf_op jit(solution)/shard_map/convert_element_type | solution.py:415

commit v4 on v3

v4 whole, which is shorter than its diff:
```python
import functools

import jax
import jax.numpy as jnp
from jax import lax
from jax.experimental import pallas as pl
from jax.experimental.pallas import tpu as pltpu
from jax.sharding import PartitionSpec as P

MESH = pl.DeviceIdType.MESH
HEAD_DIM = 256
NEG_FILL = -1e30
SCALE = HEAD_DIM ** (-0.5)
F32 = jnp.float32
BF16 = jnp.bfloat16


def nt(a, b):
    return lax.dot_general(a, b, (((1,), (1,)), ((), ())), preferred_element_type=F32)


def nn(a, b):
    return lax.dot_general(a, b, (((1,), (0,)), ((), ())), preferred_element_type=F32)


def column_of(row, count, step):
    n = row.shape[1]
    i = lax.broadcasted_iota(jnp.int32, (count, n), 0)
    j = lax.broadcasted_iota(jnp.int32, (count, n), 1)
    return jnp.sum(jnp.where(j == step * i, row, 0.0), axis=1, keepdims=True)


def kernel(
    sizes,
    q_hbm,
    k_hbm,
    v_hbm,
    docs_hbm,
    wk_hbm,
    wv_hbm,
    tq_hbm,
    out_ref,
    qv,
    kb,
    vb,
    docs,
    tq,
    w,
    enc,
    acc,
    part_out,
    part_in,
    local_sem,
    halo_s,
    halo_r,
    small_s,
    small_r,
    map_s,
    z_r,
    y_r,
    o_r,
    sib_r,
    x_s,
    x_r,
    part_s,
    part_r,
):
    n_dp, n_ctx, n_x = sizes
    n_z = n_ctx // 4
    dp = lax.axis_index("dp")
    ctx = lax.axis_index("ctx")
    x = lax.axis_index("head")
    core = lax.rem(ctx, 2)
    yl = lax.rem(ctx // 2, 2)
    z = ctx // 4
    sign = 1 - 2 * yl

    heads = k_hbm.shape[1] // HEAD_DIM
    rows = k_hbm.shape[0]
    tgts = tq_hbm.shape[0]
    crosses = wk_hbm.shape[1] // HEAD_DIM
    wrows = wk_hbm.shape[0]

    left = (dp, lax.rem(ctx + n_ctx - 1, n_ctx), x)
    right = (dp, lax.rem(ctx + 1, n_ctx), x)
    long_to = (dp, lax.rem(ctx + n_ctx - 4 * sign, n_ctx), x)
    short_to = (dp, lax.rem(ctx + n_ctx + 4 * sign, n_ctx), x)
    pair = (dp, ctx + 2 - 4 * yl, x)
    across = (lax.rem(dp + 2 * yl - 1 + n_dp, n_dp), ctx + 2 - 4 * yl, x)
    sib = (dp, ctx + 1 - 2 * core, x)
    xp = (dp, ctx, lax.rem(x + 1, n_x))
    xm = (dp, ctx, lax.rem(x + n_x - 1, n_x))

    def remote(src, dst, send, recv, device):
        return pltpu.make_async_remote_copy(
            src_ref=src, dst_ref=dst, send_sem=send, recv_sem=recv,
            device_id=device, device_id_type=MESH,
        )

    def settle(ref, sem):
        pltpu.make_async_copy(ref, ref, sem).wait()

    def settle_rows(count, sem):
        settle(w.at[0, pl.ds(0, count)], sem)

    barrier = pltpu.get_barrier_semaphore()
    partners = (left, right, long_to, short_to, pair, across, sib, xp, xm)
    for device in partners:
        pl.semaphore_signal(barrier, inc=1, device_id=device, device_id_type=MESH)

    def place(parity, e):
        return parity * n_z + (e + 3) % n_z

    def shard(parity, e):
        return pl.ds(pl.multiple_of(place(parity, e) * HEAD_DIM + core * wrows, wrows), wrows)

    own_w = []
    for n in range(crosses):
        cols = pl.ds(n * HEAD_DIM, HEAD_DIM)
        for kv, src in enumerate((wk_hbm, wv_hbm)):
            own_w.append(pltpu.make_async_copy(
                src.at[:, cols], w.at[n, shard(0, 0), pl.ds(kv * HEAD_DIM, HEAD_DIM)], local_sem.at[4]))
    copies = [
        pltpu.make_async_copy(docs_hbm, docs.at[1], local_sem.at[0]),
        pltpu.make_async_copy(q_hbm, qv, local_sem.at[1]),
        pltpu.make_async_copy(tq_hbm, tq.at[2], local_sem.at[2]),
    ]
    for h in range(heads):
        cols = pl.ds(h * HEAD_DIM, HEAD_DIM)
        copies.append(pltpu.make_async_copy(k_hbm.at[:, cols], kb.at[1, h], local_sem.at[3]))
        copies.append(pltpu.make_async_copy(v_hbm.at[:, cols], vb.at[1, h], local_sem.at[3]))
    for copy in own_w:
        copy.start()
    pl.semaphore_wait(barrier, len(partners))

    counts = {"map": 0, "sib": 0, "x": 0}

    def go(copy, kind=None):
        copy.start()
        if kind:
            counts[kind] += 1

    sides = ((left, 2), (right, 0))
    for side, (device, slot) in enumerate(sides):
        go(remote(docs_hbm, docs.at[slot], small_s.at[0], small_r.at[0], device))

    def start_halo(h):
        cols = pl.ds(h * HEAD_DIM, HEAD_DIM)
        for side, (device, slot) in enumerate(sides):
            go(remote(k_hbm.at[:, cols], kb.at[slot, h], halo_s.at[0], halo_r.at[h], device))
            go(remote(v_hbm.at[:, cols], vb.at[slot, h], halo_s.at[0], halo_r.at[h], device))

    far_y = ((2, 1), (4, 0), (5, 0))
    by_ring = ((6, 0), (6, 1), (4, 1))
    last = (2, 3, 4)
    z_pieces = [(ring, step, n) for ring, far in ((0, 5), (1, 3)) for step in range(1, far + 1)
                for n in range(crosses) if step < far or n == ring]
    y_pieces = [(e, n) for e in range(n_z) for n in range(crosses) if ((n_z - e) % n_z, n) not in by_ring]
    o_pieces = [(0, 0), (0, 1), (1, 1)]

    def send_z(ring, step, n):
        e = step - 1 if ring == 0 else 1 - step
        there = step if ring == 0 else n_z - step
        src, dst = w.at[n, shard(0, e)], w.at[n, shard(0, there)]
        go(remote(
            src, dst, map_s.at[0], z_r.at[z_pieces.index((ring, step, n))],
            long_to if ring == 0 else short_to), "map")

    def send_y(e, n):
        if (e, n) in by_ring:
            return
        there = (n_z - e) % n_z
        src, dst = w.at[n, shard(0, e)], w.at[n, shard(1, there)]
        go(remote(
            src, dst, map_s.at[0], y_r.at[y_pieces.index((there, n))],
            pair if (e, n) in far_y else across), "map")

    def send_sib(parity, e, n):
        at = w.at[n, shard(parity, e)]
        group = 1 if parity == 1 and e in last else 0
        go(remote(at, at, map_s.at[1], sib_r.at[n, group], sib), "sib")

    def arrive(ring, step, n):
        settle_rows(wrows, z_r.at[z_pieces.index((ring, step, n))])
        e = step if ring == 0 else n_z - step
        if ring == 0 and (step < 4 or (step == 4 and n == 0)):
            send_z(0, step + 1, n)
        if ring == 1 and (step < 2 or (step == 2 and n == 1)):
            send_z(1, step + 1, n)
        send_y(e, n)
        send_sib(0, e, n)

    def send_o(ring, n):
        src = w.at[n, shard(1, 1 if ring == 0 else 5)]
        dst = w.at[n, shard(1, 2 if ring == 0 else 4)]
        go(remote(
            src, dst, map_s.at[0], o_r.at[o_pieces.index((ring, n))],
            long_to if ring == 0 else short_to), "map")

    def come_o(ring, n):
        settle_rows(wrows, o_r.at[o_pieces.index((ring, n))])
        send_sib(1, 2 if ring == 0 else 4, n)

    def come_y(e, n):
        settle_rows(wrows, y_r.at[y_pieces.index((e, n))])
        send_sib(1, e, n)

    start_halo(0)
    for copy in copies:
        copy.start()
    settle_rows(crosses * wrows, local_sem.at[4])
    for n in range(crosses):
        send_z(0, 1, n)
        send_z(1, 1, n)
        send_y(0, n)
    for h in range(1, heads):
        start_halo(h)
    for n in range(crosses):
        send_sib(0, 0, n)
    for side, (device, slot) in enumerate(sides):
        go(remote(tq_hbm, tq.at[1 - side], small_s.at[1], small_r.at[1], device))

    for copy in copies[:3]:
        copy.wait()
    settle_rows(2 * heads * rows // 2, local_sem.at[3])
    settle(docs.at[0:2], small_r.at[0])

    marks = [docs[slot].astype(F32) for slot in range(3)]
    own_col = column_of(marks[1], rows, 1)
    tgt_col = [column_of(marks[slot], tgts, rows // tgts) for slot in range(3)]
    side_col = jnp.concatenate([tgt_col[0], tgt_col[2]], axis=0)

    def enc_cols(at_x, h):
        e = lax.rem(sign * (at_x * 2 + h // 2 - z) + 2 * n_z + 3, n_z)
        parity = yl if h % 2 == 0 else 1 - yl
        return pl.ds(pl.multiple_of((parity * n_z + e) * HEAD_DIM, HEAD_DIM), HEAD_DIM)

    def half_rows(half):
        return pl.ds(half * (rows // 2), rows // 2)

    def attend(h):
        settle_rows(2 * rows, halo_r.at[h])
        query = qv[:, h * HEAD_DIM:(h + 1) * HEAD_DIM]
        scores = []
        for slot in range(3):
            raw = nt(query, kb[slot, h]) * SCALE
            scores.append(jnp.where(own_col == marks[slot], raw, NEG_FILL))
        top = jnp.max(jnp.maximum(jnp.maximum(scores[0], scores[1]), scores[2]), axis=1, keepdims=True)
        weights = [jnp.exp(s - top) for s in scores]
        total = jnp.sum(weights[0] + weights[1] + weights[2], axis=1, keepdims=True)
        summed = sum(nn(weights[slot].astype(BF16), vb[slot, h]) for slot in range(3))
        at = enc_cols(x, h)
        enc[:, at] = (summed / total).astype(BF16)
        for part in range(2):
            for side, device in enumerate((xp, xm)):
                piece = enc.at[half_rows(part if side == 0 else 1 - part), at]
                go(remote(piece, piece, x_s.at[0], x_r.at[h if part == 0 else heads], device), "x")

    def hand_on(h):
        settle_rows(rows // 2, x_r.at[h])
        for side, device in enumerate((xp, xm)):
            source = lax.rem(x + n_x - 1, n_x) if side == 0 else lax.rem(x + 1, n_x)
            at = enc_cols(source, h)
            piece = enc.at[half_rows(side), at]
            go(remote(piece, piece, x_s.at[0], x_r.at[heads], device), "x")

    arrive(0, 1, 0)
    come_y(0, 0)
    arrive(0, 1, 1)
    attend(0)
    come_y(0, 1)
    arrive(1, 1, 0)
    arrive(0, 2, 0)
    come_y(7, 0)
    arrive(0, 2, 1)
    arrive(1, 1, 1)
    attend(1)
    hand_on(0)
    come_y(7, 1)
    arrive(0, 3, 0)
    arrive(0, 3, 1)
    arrive(1, 2, 0)
    attend(2)
    hand_on(1)
    come_y(1, 0)
    come_y(6, 0)
    arrive(0, 4, 0)
    send_o(0, 0)
    arrive(0, 4, 1)
    arrive(1, 2, 1)
    attend(3)
    hand_on(2)
    come_y(1, 1)
    send_o(0, 1)
    arrive(0, 5, 0)
    come_y(5, 0)
    come_y(5, 1)
    send_o(1, 1)
    hand_on(3)
    arrive(1, 3, 1)
    come_y(6, 1)
    come_o(0, 0)
    come_y(4, 0)

    settle_rows(heads * rows, x_r.at[heads])

    split = (2 * n_z - len(last)) * HEAD_DIM

    def maps_most(n):
        settle_rows((2 * n_z - len(last)) * wrows, sib_r.at[n, 0])
        acc[n] = nn(enc[:, :split], w[n, :split])

    def maps_rest(n):
        settle_rows(len(last) * wrows, sib_r.at[n, 1])
        both = (acc[n] + nn(enc[:, split:], w[n, split:])).astype(BF16)
        return both[:, :HEAD_DIM], both[:, HEAD_DIM:]

    def partial_sums(query, col, memory):
        raw = nt(query, memory[0]) * SCALE
        scores = jnp.where(col == marks[1], raw, NEG_FILL)
        top = jnp.max(scores, axis=1, keepdims=True)
        weights = jnp.exp(scores - top)
        total = jnp.sum(weights, axis=1, keepdims=True)
        return top, total, nn(weights.astype(BF16), memory[1])

    diagonal = lax.broadcasted_iota(jnp.int32, (tgts, HEAD_DIM), 0) == lax.broadcasted_iota(
        jnp.int32, (tgts, HEAD_DIM), 1)
    first_row = lax.broadcasted_iota(jnp.int32, (8, HEAD_DIM), 0) == 0

    def row_of(column):
        return jnp.sum(jnp.where(diagonal, column, 0.0), axis=0, keepdims=True)

    def give(n, memory):
        query = tq[0:2, :, n * HEAD_DIM:(n + 1) * HEAD_DIM].reshape(2 * tgts, HEAD_DIM)
        top, total, summed = partial_sums(query, side_col, memory)
        for side in range(2):
            at = slice(side * tgts, (side + 1) * tgts)
            part_out[side, n, 0:tgts] = summed[at]
            part_out[side, n, tgts:] = jnp.where(first_row, row_of(top[at]), row_of(total[at]))
            go(remote(part_out.at[side, n], part_in.at[1 - side, n], part_s.at[0], part_r.at[n], sides[side][0]))

    def merge(n, own):
        settle(part_in.at[:, n], part_r.at[n])
        tops, totals, sums = [own[0]], [own[1]], [own[2]]
        for side in range(2):
            tops.append(column_of(part_in[1 - side, n, tgts:tgts + 1], tgts, 1))
            totals.append(column_of(part_in[1 - side, n, tgts + 1:tgts + 2], tgts, 1))
            sums.append(part_in[1 - side, n, 0:tgts])
        most = jnp.maximum(jnp.maximum(tops[0], tops[1]), tops[2])
        factor = [jnp.exp(t - most) for t in tops]
        total = sum(f * t for f, t in zip(factor, totals))
        summed = sum(f * s for f, s in zip(factor, sums))
        out_ref[:, n * HEAD_DIM:(n + 1) * HEAD_DIM] = summed / total

    settle(tq.at[0:2], small_r.at[1])
    maps_most(0)
    come_y(3, 0)
    come_o(0, 1)
    come_o(1, 1)
    come_y(3, 1)
    maps_most(1)
    memory = {}
    for n in range(crosses):
        memory[n] = maps_rest(n)
        give(n, memory[n])
    own = [
        partial_sums(tq[2, :, n * HEAD_DIM:(n + 1) * HEAD_DIM], tgt_col[1], memory[n]) for n in range(crosses)
    ]
    for n in range(crosses):
        merge(n, own[n])

    settle(docs.at[0:2], small_s.at[0])
    settle(tq.at[0:2], small_s.at[1])
    settle(part_out, part_s.at[0])
    settle_rows(2 * heads * rows, halo_s.at[0])
    settle_rows(counts["x"] * rows // 4, x_s.at[0])
    settle_rows(counts["map"] * wrows, map_s.at[0])
    settle_rows(counts["sib"] * wrows, map_s.at[1])


def on_device(sizes, enc_query, enc_key, enc_value, doc_ids, key_map, value_map, tgt_query):
    rows, width = enc_key.shape
    heads = width // HEAD_DIM
    wrows, wcols = key_map.shape
    crosses = wcols // HEAD_DIM
    tgts = tgt_query.shape[0]
    n_z = sizes[1] // 4
    docs = doc_ids.reshape(1, rows)
    dma = pltpu.SemaphoreType.DMA
    any_spec = pl.BlockSpec(memory_space=pl.ANY)
    out = pl.pallas_call(
        functools.partial(kernel, sizes),
        out_shape=pltpu.VMEM((tgts, wcols), F32),
        in_specs=[any_spec] * 7,
        out_specs=pl.BlockSpec(memory_space=pltpu.VMEM),
        scratch_shapes=[
            pltpu.VMEM((rows, width), BF16),
            pltpu.VMEM((3, heads, rows, HEAD_DIM), BF16),
            pltpu.VMEM((3, heads, rows, HEAD_DIM), BF16),
            pltpu.VMEM((3, 1, rows), jnp.int32),
            pltpu.VMEM((3, tgts, wcols), BF16),
            pltpu.VMEM((crosses, wrows * sizes[1], 2 * HEAD_DIM), BF16),
            pltpu.VMEM((rows, width * sizes[2]), BF16),
            pltpu.VMEM((crosses, rows, 2 * HEAD_DIM), F32),
            pltpu.VMEM((2, crosses, tgts + 8, HEAD_DIM), F32),
            pltpu.VMEM((2, crosses, tgts + 8, HEAD_DIM), F32),
            dma((5,)),
            dma((1,)),
            dma((heads,)),
            dma((2,)),
            dma((2,)),
            dma((2,)),
            dma((14,)),
            dma((13,)),
            dma((3,)),
            dma((crosses, 2)),
            dma((1,)),
            dma((heads + 1,)),
            dma((1,)),
            dma((crosses,)),
        ],
        compiler_params=pltpu.CompilerParams(
            collective_id=0, has_side_effects=True, vmem_limit_bytes=60 * 1024 * 1024
        ),
    )(enc_query, enc_key, enc_value, docs, key_map, value_map, tgt_query)
    return out.astype(BF16)


def solution(mesh):
    sizes = (mesh.shape["dp"], mesh.shape["ctx"], mesh.shape["head"])
    in_specs = (
        P(("dp", "ctx"), "head"),
        P(("dp", "ctx"), "head"),
        P(("dp", "ctx"), "head"),
        P(("dp", "ctx")),
        P("ctx", "head"),
        P("ctx", "head"),
        P(("dp", "ctx"), "head"),
    )
    return jax.shard_map(
        functools.partial(on_device, sizes),
        mesh=mesh,
        in_specs=in_specs,
        out_specs=P(("dp", "ctx"), "head"),
        check_vma=False,
    )
```

time: 60.1 us -> 56.3 us (0.937); the launches traced: 59.1 us -> 56.1 us
  Pallas kernels: 57.5 us -> 55.4 us
  other arithmetic: 1.54 us -> 0.64 us
    pallas_call x1, Pallas kernels: 57.5 us -> 55.4 us  [on_device(): pl.pallas_call(functools.partial(kernel, sizes), out_shape=pltpu.VMEM((tg...]
    convert_element_type x1, other arithmetic: 1.54 us -> 0.64 us  [on_device(): return out.astype(BF16)]
where the time goes in v4:
time: 56.3 us; the launch traced here: 56.1 us
  Pallas kernels  55.4 us (98%)
  other arithmetic  0.64 us (1%)
    pallas_call x1, Pallas kernels, on_device(): pl.pallas_call(functools.partial(kernel, sizes), out_shape=pltpu.VMEM((tg...  55.4 us

profile of v4, /device:TPU:1, one launch (start us, length us, event | category | flops | bytes accessed | tf_op | source)
XLA Modules:
  0.0 56.1 jit_solution(6785178963203414679)
XLA Ops:
  0.0 55.4 %shard_map.73 = f32[64,512]{1,0:T(8,128)S(1)} custom-call(bf16[256,1024]{1,0:T(8,128)(2,1)} %q_hbm.1, bf16[256,1024]{1,0:T(8,128)(2,1)} %k_hbm.1, bf16[256,1024]{1,0:T(8,128)(2,1)} %v_hbm.1, s32[1,256]{1,0:T(1,128)} %bitcast.1, bf16[128,512]{1,0:T(8,128)(2,1)} %wk_hbm.1, bf16[128,512]{1,0:T(8,128)(2,1)} %wv_hbm.1, bf16[64,512]{1,0:T(8,128)(2,1)} %tq_hbm.1), custom_call_target="tpu_custom_call" | custom-call | tf_op jit(solution)/shard_map/pallas_call | solution.py:391
  55.4 0.6 %convert_element_type.3 = bf16[64,512]{1,0:T(8,128)(2,1)} convert(f32[64,512]{1,0:T(8,128)S(1)} %shard_map.73) | non-fusion elementwise | flops 32768 | bytes 196608 | tf_op jit(solution)/shard_map/convert_element_type | solution.py:426

commit v5 on v4

--- a/solution.py
+++ b/solution.py
@@ -50,6 +50,8 @@
     acc,
     part_out,
     part_in,
+    stat_out,
+    stat_in,
     local_sem,
     halo_s,
     halo_r,
@@ -64,6 +66,8 @@
     x_r,
     part_s,
     part_r,
+    stat_s,
+    stat_r,
 ):
     n_dp, n_ctx, n_x = sizes
     n_z = n_ctx // 4
@@ -150,7 +154,8 @@
             go(remote(k_hbm.at[:, cols], kb.at[slot, h], halo_s.at[0], halo_r.at[h], device))
             go(remote(v_hbm.at[:, cols], vb.at[slot, h], halo_s.at[0], halo_r.at[h], device))
 
-    far_y = ((2, 1), (4, 0), (5, 0))
+    far_y = ((4, 0), (5, 0))
+    held_back = ((2, 1), (4, 0))
     by_ring = ((6, 0), (6, 1), (4, 1))
     last = (2, 3, 4)
     z_pieces = [(ring, step, n) for ring, far in ((0, 5), (1, 3)) for step in range(1, far + 1)
@@ -187,7 +192,8 @@
             send_z(0, step + 1, n)
         if ring == 1 and (step < 2 or (step == 2 and n == 1)):
             send_z(1, step + 1, n)
-        send_y(e, n)
+        if (e, n) not in held_back:
+            send_y(e, n)
         send_sib(0, e, n)
 
     def send_o(ring, n):
@@ -217,8 +223,6 @@
         start_halo(h)
     for n in range(crosses):
         send_sib(0, 0, n)
-    for side, (device, slot) in enumerate(sides):
-        go(remote(tq_hbm, tq.at[1 - side], small_s.at[1], small_r.at[1], device))
 
     for copy in copies[:3]:
         copy.wait()
@@ -264,6 +268,10 @@
             piece = enc.at[half_rows(side), at]
             go(remote(piece, piece, x_s.at[0], x_r.at[heads], device), "x")
 
+    def send_targets():
+        for side in range(2):
+            go(remote(tq_hbm, tq.at[1 - side], small_s.at[1], small_r.at[1], sides[side][0]))
+
     arrive(0, 1, 0)
     come_y(0, 0)
     arrive(0, 1, 1)
@@ -279,6 +287,7 @@
     come_y(7, 1)
     arrive(0, 3, 0)
     arrive(0, 3, 1)
+    send_y(2, 1)
     arrive(1, 2, 0)
     attend(2)
     hand_on(1)
@@ -288,7 +297,9 @@
     send_o(0, 0)
     arrive(0, 4, 1)
     arrive(1, 2, 1)
+    send_y(4, 0)
     attend(3)
+    send_targets()
     hand_on(2)
     come_y(1, 1)
     send_o(0, 1)
@@ -298,9 +309,9 @@
     send_o(1, 1)
     hand_on(3)
     arrive(1, 3, 1)
+    come_y(4, 0)
+    come_o(0, 0)
     come_y(6, 1)
-    come_o(0, 0)
-    come_y(4, 0)
 
     settle_rows(heads * rows, x_r.at[heads])
 
@@ -335,17 +346,19 @@
         top, total, summed = partial_sums(query, side_col, memory)
         for side in range(2):
             at = slice(side * tgts, (side + 1) * tgts)
-            part_out[side, n, 0:tgts] = summed[at]
-            part_out[side, n, tgts:] = jnp.where(first_row, row_of(top[at]), row_of(total[at]))
+            part_out[side, n] = summed[at].astype(BF16)
+            stat_out[side, n] = jnp.where(first_row, row_of(top[at]), row_of(total[at]))
             go(remote(part_out.at[side, n], part_in.at[1 - side, n], part_s.at[0], part_r.at[n], sides[side][0]))
+            go(remote(stat_out.at[side, n], stat_in.at[1 - side, n], stat_s.at[0], stat_r.at[n], sides[side][0]))
 
     def merge(n, own):
+        settle(stat_in.at[:, n], stat_r.at[n])
         settle(part_in.at[:, n], part_r.at[n])
         tops, totals, sums = [own[0]], [own[1]], [own[2]]
         for side in range(2):
-            tops.append(column_of(part_in[1 - side, n, tgts:tgts + 1], tgts, 1))
-            totals.append(column_of(part_in[1 - side, n, tgts + 1:tgts + 2], tgts, 1))
-            sums.append(part_in[1 - side, n, 0:tgts])
+            tops.append(column_of(stat_in[1 - side, n, 0:1], tgts, 1))
+            totals.append(column_of(stat_in[1 - side, n, 1:2], tgts, 1))
+            sums.append(part_in[1 - side, n].astype(F32))
         most = jnp.maximum(jnp.maximum(tops[0], tops[1]), tops[2])
         factor = [jnp.exp(t - most) for t in tops]
         total = sum(f * t for f, t in zip(factor, totals))
@@ -372,6 +385,7 @@
     settle(docs.at[0:2], small_s.at[0])
     settle(tq.at[0:2], small_s.at[1])
     settle(part_out, part_s.at[0])
+    settle(stat_out, stat_s.at[0])
     settle_rows(2 * heads * rows, halo_s.at[0])
     settle_rows(counts["x"] * rows // 4, x_s.at[0])
     settle_rows(counts["map"] * wrows, map_s.at[0])
@@ -402,8 +416,10 @@
             pltpu.VMEM((crosses, wrows * sizes[1], 2 * HEAD_DIM), BF16),
             pltpu.VMEM((rows, width * sizes[2]), BF16),
             pltpu.VMEM((crosses, rows, 2 * HEAD_DIM), F32),
-            pltpu.VMEM((2, crosses, tgts + 8, HEAD_DIM), F32),
-            pltpu.VMEM((2, crosses, tgts + 8, HEAD_DIM), F32),
+            pltpu.VMEM((2, crosses, tgts, HEAD_DIM), BF16),
+            pltpu.VMEM((2, crosses, tgts, HEAD_DIM), BF16),
+            pltpu.VMEM((2, crosses, 8, HEAD_DIM), F32),
+            pltpu.VMEM((2, crosses, 8, HEAD_DIM), F32),
             dma((5,)),
             dma((1,)),
             dma((heads,)),
@@ -416,6 +432,8 @@
             dma((crosses, 2)),
             dma((1,)),
             dma((heads + 1,)),
+            dma((1,)),
+            dma((crosses,)),
             dma((1,)),
             dma((crosses,)),
         ],

time: 56.3 us -> 55.5 us (0.986)
  Pallas kernels: 55.4 us -> 54.4 us
    pallas_call x1, Pallas kernels: 55.4 us -> 54.4 us  [on_device(): pl.pallas_call(functools.partial(kernel, sizes), out_shape=pltpu.VMEM((tg...]
where the time goes in v5:
time: 55.5 us; the launch traced here: 55 us
  Pallas kernels  54.4 us (98%)
  other arithmetic  0.64 us (1%)
    pallas_call x1, Pallas kernels, on_device(): pl.pallas_call(functools.partial(kernel, sizes), out_shape=pltpu.VMEM((tg...  54.4 us

profile of v5, /device:TPU:1, one launch (start us, length us, event | category | flops | bytes accessed | tf_op | source)
XLA Modules:
  0.0 55.0 jit_solution(11791799176095502541)
XLA Ops:
  0.0 54.4 %shard_map.73 = f32[64,512]{1,0:T(8,128)S(1)} custom-call(bf16[256,1024]{1,0:T(8,128)(2,1)} %q_hbm.1, bf16[256,1024]{1,0:T(8,128)(2,1)} %k_hbm.1, bf16[256,1024]{1,0:T(8,128)(2,1)} %v_hbm.1, s32[1,256]{1,0:T(1,128)} %bitcast.1, bf16[128,512]{1,0:T(8,128)(2,1)} %wk_hbm.1, bf16[128,512]{1,0:T(8,128)(2,1)} %wv_hbm.1, bf16[64,512]{1,0:T(8,128)(2,1)} %tq_hbm.1), custom_call_target="tpu_custom_call" | custom-call | tf_op jit(solution)/shard_map/pallas_call | solution.py:405
  54.4 0.6 %convert_element_type.3 = bf16[64,512]{1,0:T(8,128)(2,1)} convert(f32[64,512]{1,0:T(8,128)S(1)} %shard_map.73) | non-fusion elementwise | flops 32768 | bytes 196608 | tf_op jit(solution)/shard_map/convert_element_type | solution.py:444

commit v6 on v5

--- a/solution.py
+++ b/solution.py
@@ -137,7 +137,7 @@
         copy.start()
     pl.semaphore_wait(barrier, len(partners))
 
-    counts = {"map": 0, "sib": 0, "x": 0}
+    counts = {"map": 0, "sib": 0}
 
     def go(copy, kind=None):
         copy.start()
@@ -239,8 +239,11 @@
         parity = yl if h % 2 == 0 else 1 - yl
         return pl.ds(pl.multiple_of((parity * n_z + e) * HEAD_DIM, HEAD_DIM), HEAD_DIM)
 
-    def half_rows(half):
-        return pl.ds(half * (rows // 2), rows // 2)
+    half, quarter = rows // 2, rows // 4
+    pieces = (
+        (pl.ds(0, quarter), pl.ds(quarter, quarter), pl.ds(half, half)),
+        (pl.ds(half, quarter), pl.ds(half + quarter, quarter), pl.ds(0, half)),
+    )
 
     def attend(h):
         settle_rows(2 * rows, halo_r.at[h])
@@ -255,18 +258,18 @@
         summed = sum(nn(weights[slot].astype(BF16), vb[slot, h]) for slot in range(3))
         at = enc_cols(x, h)
         enc[:, at] = (summed / total).astype(BF16)
+        for part in range(3):
+            for side, device in enumerate((xp, xm)):
+                piece = enc.at[pieces[side][part], at]
+                go(remote(piece, piece, x_s.at[0], x_r.at[2 * h + part if part < 2 else 2 * heads], device))
+
+    def hand_on(h):
         for part in range(2):
+            settle_rows(quarter, x_r.at[2 * h + part])
             for side, device in enumerate((xp, xm)):
-                piece = enc.at[half_rows(part if side == 0 else 1 - part), at]
-                go(remote(piece, piece, x_s.at[0], x_r.at[h if part == 0 else heads], device), "x")
-
-    def hand_on(h):
-        settle_rows(rows // 2, x_r.at[h])
-        for side, device in enumerate((xp, xm)):
-            source = lax.rem(x + n_x - 1, n_x) if side == 0 else lax.rem(x + 1, n_x)
-            at = enc_cols(source, h)
-            piece = enc.at[half_rows(side), at]
-            go(remote(piece, piece, x_s.at[0], x_r.at[heads], device), "x")
+                source = lax.rem(x + n_x - 1, n_x) if side == 0 else lax.rem(x + 1, n_x)
+                piece = enc.at[pieces[side][part], enc_cols(source, h)]
+                go(remote(piece, piece, x_s.at[0], x_r.at[2 * heads], device))
 
     def send_targets():
         for side in range(2):
@@ -312,8 +315,10 @@
     come_y(4, 0)
     come_o(0, 0)
     come_y(6, 1)
-
-    settle_rows(heads * rows, x_r.at[heads])
+    come_o(0, 1)
+    come_y(3, 0)
+
+    settle_rows(heads * rows, x_r.at[2 * heads])
 
     split = (2 * n_z - len(last)) * HEAD_DIM
 
@@ -367,11 +372,9 @@
 
     settle(tq.at[0:2], small_r.at[1])
     maps_most(0)
-    come_y(3, 0)
-    come_o(0, 1)
     come_o(1, 1)
+    maps_most(1)
     come_y(3, 1)
-    maps_most(1)
     memory = {}
     for n in range(crosses):
         memory[n] = maps_rest(n)
@@ -387,7 +390,7 @@
     settle(part_out, part_s.at[0])
     settle(stat_out, stat_s.at[0])
     settle_rows(2 * heads * rows, halo_s.at[0])
-    settle_rows(counts["x"] * rows // 4, x_s.at[0])
+    settle_rows(3 * heads * rows // 2, x_s.at[0])
     settle_rows(counts["map"] * wrows, map_s.at[0])
     settle_rows(counts["sib"] * wrows, map_s.at[1])
 
@@ -431,7 +434,7 @@
             dma((3,)),
             dma((crosses, 2)),
             dma((1,)),
-            dma((heads + 1,)),
+            dma((2 * heads + 1,)),
             dma((1,)),
             dma((crosses,)),
             dma((1,)),

time: 55.5 us -> 55.7 us (level)
  no operation moved by 1% of the time
where the time goes in v6:
time: 55.7 us; the launch traced here: 54.8 us
  Pallas kernels  54.1 us (97%)
  other arithmetic  0.64 us (1%)
    pallas_call x1, Pallas kernels, on_device(): pl.pallas_call(functools.partial(kernel, sizes), out_shape=pltpu.VMEM((tg...  54.1 us

profile of v6, /device:TPU:1, one launch (start us, length us, event | category | flops | bytes accessed | tf_op | source)
XLA Modules:
  0.0 54.8 jit_solution(4866238531025994997)
XLA Ops:
  0.0 54.1 %shard_map.73 = f32[64,512]{1,0:T(8,128)S(1)} custom-call(bf16[256,1024]{1,0:T(8,128)(2,1)} %q_hbm.1, bf16[256,1024]{1,0:T(8,128)(2,1)} %k_hbm.1, bf16[256,1024]{1,0:T(8,128)(2,1)} %v_hbm.1, s32[1,256]{1,0:T(1,128)} %bitcast.1, bf16[128,512]{1,0:T(8,128)(2,1)} %wk_hbm.1, bf16[128,512]{1,0:T(8,128)(2,1)} %wv_hbm.1, bf16[64,512]{1,0:T(8,128)(2,1)} %tq_hbm.1), custom_call_target="tpu_custom_call" | custom-call | tf_op jit(solution)/shard_map/pallas_call | solution.py:408
  54.1 0.6 %convert_element_type.3 = bf16[64,512]{1,0:T(8,128)(2,1)} convert(f32[64,512]{1,0:T(8,128)S(1)} %shard_map.73) | non-fusion elementwise | flops 32768 | bytes 196608 | tf_op jit(solution)/shard_map/convert_element_type | solution.py:447
